TPU v7x, 512 devices: a whole 4x4x16 slice. The times are simulated.
512 devices in a mesh: row: 32 (over x, y, core), col: 16 (over z).
Axes of the slice: x: 4, y: 4, z: 16, core: 2. Of those that a mesh axis runs over, the one named last changes fastest.
Arguments:
- mixture_fractions: float32 [54, 256, 2048], P(None, 'row', 'col'), may hold values from -6 to 6
- spreading_coefficient: float32 [256, 2048], P('row', 'col'), may hold values from 0.02 to 0.12
- flow_speed_vector: float32 [2, 256, 2048], P(None, 'row', 'col'), may hold values from -0.15 to 0.15
- thermal_state: float32 [256, 2048], P('row', 'col'), may hold values from -6 to 6
- chemistry_active_indicator: int32 [256, 2048], P('row', 'col'), may hold values from 0 to 1, as said below
- entry_level_matrix: bfloat16 [256, 55], replicated, may hold values from -0.875 to 0.875
- entry_level_offset: float32 [256], replicated, may hold values from -3 to 3
- hidden_level_matrix: bfloat16 [256, 256], replicated, may hold values from -0.375 to 0.375
- hidden_level_offset: float32 [256], replicated, may hold values from -3 to 3
- final_level_matrix: bfloat16 [54, 256], replicated, may hold values from -0.375 to 0.375
- final_level_offset: float32 [54], replicated, may hold values from -3 to 3
Outputs:
- species_next: float32 [54, 256, 2048], P(None, 'row', 'col')
Inputs may be any that keep to these rules, and one draw needn't show every extreme that they name: `chemistry_active_indicator`: split the grid into tiles of 8 x 128 cells and bands of 8 rows. Every tile holds at most 384 flagged cells, and in every band some tile holds exactly 384; every band holds exactly 2048 flagged cells.
All inputs are finite; a program needn't handle non-finite values.
Results may differ from a plain program's by a relative error of at most 0.0003.
Values sent between devices are 32-bit elements; how exact they have to be, the bound alone decides.
No kernel may reach another device: no remote copies, remote signals or barrier semaphores. Data moves between devices by JAX's collectives and lax.ppermute only.
A program may use at most 64 MiB of HBM per device.

v0:
```python
import jax
import jax.numpy as jnp
from jax import lax
from jax.sharding import PartitionSpec as P

SUBSTEPS = 8
TRANSPORT_STEPS = 3


time_step = 1.0
chem_step = 0.0625


def padded_2(array, sides, width):
    edges = {}
    for axis, dim in sides:
        devices, length = (lax.axis_size(axis), array.shape[dim])
        up = [(i, (i + 1) % devices) for i in range(devices - 1)]
        last = lax.slice_in_dim(array, length - width, length, axis=dim)
        initial = lax.slice_in_dim(array, 0, width, axis=dim)
        edges[dim] = (
            lax.ppermute(last, axis, up),
            lax.ppermute(initial, axis, [(b, a) for a, b in up]),
        )
    done = []
    for _, dim in sides:
        low, high = edges[dim]
        around = [(width, width) if d in done else (0, 0) for d in range(array.ndim)]
        array = jnp.concatenate([jnp.pad(low, around), array, jnp.pad(high, around)], axis=dim)
        done.append(dim)
    return array


def advance(padded, pad_diff, speed_cols, speed_rows):
    left_vals = padded[..., 1:-1, :-1]
    right_vals = padded[..., 1:-1, 1:]
    face_diff = 0.5 * (pad_diff[1:-1, :-1] + pad_diff[1:-1, 1:])
    face_speed = 0.5 * (speed_cols[1:-1, :-1] + speed_cols[1:-1, 1:])
    flux_cols = face_diff * (right_vals - left_vals) - (
        jnp.maximum(face_speed, 0.0) * left_vals + jnp.minimum(face_speed, 0.0) * right_vals
    )
    lower_vals = padded[..., :-1, 1:-1]
    upper_vals = padded[..., 1:, 1:-1]
    face_diff = 0.5 * (pad_diff[:-1, 1:-1] + pad_diff[1:, 1:-1])
    face_speed = 0.5 * (speed_rows[:-1, 1:-1] + speed_rows[1:, 1:-1])
    flux_rows = face_diff * (upper_vals - lower_vals) - (
        jnp.maximum(face_speed, 0.0) * lower_vals + jnp.minimum(face_speed, 0.0) * upper_vals
    )
    change = (
        flux_cols[..., 1:] - flux_cols[..., :-1] + flux_rows[..., 1:, :] - flux_rows[..., :-1, :]
    )
    return padded[..., 1:-1, 1:-1] + time_step * change


def network(
    inputs,
    entry_level_matrix,
    entry_level_offset,
    hidden_level_matrix,
    hidden_level_offset,
    final_level_matrix,
    final_level_offset,
):
    hidden = jnp.tanh(
        jnp.dot(entry_level_matrix, inputs, preferred_element_type=jnp.float32)
        + entry_level_offset[:, None]
    ).astype(jnp.bfloat16)
    hidden = jnp.tanh(
        jnp.dot(hidden_level_matrix, hidden, preferred_element_type=jnp.float32)
        + hidden_level_offset[:, None]
    ).astype(jnp.bfloat16)
    return (
        jnp.dot(final_level_matrix, hidden, preferred_element_type=jnp.float32)
        + final_level_offset[:, None]
    )


def integrate(
    state,
    heat,
    entry_level_matrix,
    entry_level_offset,
    hidden_level_matrix,
    hidden_level_offset,
    final_level_matrix,
    final_level_offset,
):
    total = jnp.zeros(state.shape, jnp.float32)
    for index in range(SUBSTEPS):
        inputs = jnp.concatenate([state + chem_step * total, heat[None]], 0).astype(jnp.bfloat16)
        total = total + network(
            inputs,
            entry_level_matrix,
            entry_level_offset,
            hidden_level_matrix,
            hidden_level_offset,
            final_level_matrix,
            final_level_offset,
        )
    return chem_step * total


def species_halo(field):
    return padded_2(field, (("row", 1), ("col", 2)), 1)


def shards(
    mixture_fractions,
    spreading_coefficient,
    flow_speed_vector,
    thermal_state,
    chemistry_active_indicator,
    entry_level_matrix,
    entry_level_offset,
    hidden_level_matrix,
    hidden_level_offset,
    final_level_matrix,
    final_level_offset,
):
    species_count, tile_rows, tile_cols = mixture_fractions.shape
    cell_total = tile_rows * tile_cols
    cell_capacity = 3 * (cell_total // 8)
    coefficients = jnp.concatenate([spreading_coefficient[None], flow_speed_vector], 0)
    coefficients = padded_2(coefficients, (("row", 1), ("col", 2)), 1)
    carried_quantity = mixture_fractions
    for section in range(TRANSPORT_STEPS):
        padded = species_halo(carried_quantity)
        carried_quantity = advance(padded, coefficients[0], coefficients[1], coefficients[2])
    predictor_vector = jnp.concatenate([carried_quantity, thermal_state[None]], 0).reshape(
        species_count + 1, cell_total
    )
    active = chemistry_active_indicator.reshape(-1)
    place = jnp.cumsum(active) - 1
    slot_cell = (
        jnp.zeros((cell_capacity + 1,), jnp.int32)
        .at[jnp.where(active == 1, place, cell_capacity)]
        .set(jnp.arange(cell_total, dtype=jnp.int32))[:cell_capacity]
    )
    active_total = jnp.sum(active)
    filled = jnp.arange(cell_capacity, dtype=jnp.int32) < active_total
    gathered = predictor_vector[:, slot_cell]
    slot_rates = integrate(
        gathered[:species_count],
        gathered[species_count],
        entry_level_matrix,
        entry_level_offset,
        hidden_level_matrix,
        hidden_level_offset,
        final_level_matrix,
        final_level_offset,
    )
    target = jnp.where(filled, slot_cell, cell_total)
    increments = (
        jnp.zeros((species_count, cell_total + 1), jnp.float32)
        .at[:, target]
        .add(slot_rates)[:, :cell_total]
    )
    species_next = carried_quantity.reshape(species_count, cell_total) + increments
    return species_next.reshape(species_count, tile_rows, tile_cols)


def solution(mesh):
    in_specs = (
        P(None, "row", "col"),
        P("row", "col"),
        P(None, "row", "col"),
        P("row", "col"),
        P("row", "col"),
        P(),
        P(),
        P(),
        P(),
        P(),
        P(),
    )
    out_specs = P(None, "row", "col")
    return jax.shard_map(shards, mesh=mesh, in_specs=in_specs, out_specs=out_specs, check_vma=False)
```

profile of v0, /device:TPU:386, one launch (start us, length us, event | category | flops | bytes accessed | tf_op | source)
XLA Modules:
  0.0 96.2 jit_solution(14049005423172456946)
XLA Ops:
  0.0 0.9 fusion.99
  0.9 2.9 %collective-permute-start = (f32[3,8,1]{2,1,0:T(8,128)S(1)}, f32[3,8,1]{2,1,0:T(8,128)S(1)}, u32[]{:S(2)}, u32[]{:S(2)}) collective-permute-start(f32[3,8,1]{2,1,0:T(8,128)S(1)} %get-tuple-element.26), channel_id=1, source_target_pairs={{0,1},{1,2},{2,3},{3,4},{4,5},{5,6},{6,7},{7,8},{8,9},{9,10},{10,1... | collective-permute-start | bytes 296 | tf_op jit(solution)/shard_map/ppermute | solution.py:22
  3.8 4.1 %collective-permute-start.3 = (f32[3,8,1]{2,1,0:T(8,128)S(1)}, f32[3,8,1]{2,1,0:T(8,128)S(1)}, u32[]{:S(2)}, u32[]{:S(2)}) collective-permute-start(f32[3,8,1]{2,1,0:T(8,128)S(1)} %get-tuple-element.27), channel_id=1, source_target_pairs={{1,0},{2,1},{3,2},{4,3},{5,4},{6,5},{7,6},{8,7},{9,8},{10,9},{11,1... | collective-permute-start | bytes 296 | tf_op jit(solution)/shard_map/ppermute | solution.py:23
  8.0 1.9 %collective-permute-start.1 = (f32[3,1,128]{2,1,0:T(1,128)S(1)}, f32[3,1,128]{2,1,0:T(1,128)S(1)}, u32[]{:S(2)}, u32[]{:S(2)}) collective-permute-start(f32[3,1,128]{2,1,0:T(1,128)S(1)} %get-tuple-element.24), channel_id=1, source_target_pairs={{0,16},{16,32},{32,48},{48,64},{64,80},{80,96},{96,112},{112,128},... | collective-permute-start | bytes 4616 | tf_op jit(solution)/shard_map/ppermute | solution.py:22
  9.9 5.8 %collective-permute-start.2 = (f32[3,1,128]{2,1,0:T(1,128)S(1)}, f32[3,1,128]{2,1,0:T(1,128)S(1)}, u32[]{:S(2)}, u32[]{:S(2)}) collective-permute-start(f32[3,1,128]{2,1,0:T(1,128)S(1)} %get-tuple-element.25), channel_id=1, source_target_pairs={{16,0},{32,16},{48,32},{64,48},{80,64},{96,80},{112,96},{128,112},... | collective-permute-start | bytes 4616 | tf_op jit(solution)/shard_map/ppermute | solution.py:23
  15.7 1.1 %fusion.131 = (f32[54,1,128]{2,1,0:T(1,128)S(1)}, f32[54,1,128]{2,1,0:T(1,128)S(1)}) fusion(f32[54,8,128]{2,1,0:T(8,128)} %param.11), kind=kLoop, calls=%fused_computation.224 | loop fusion | bytes 110592 | tf_op jit(solution)/shard_map/slice | solution.py:19
  16.8 2.1 %collective-permute-start.4 = (f32[54,1,128]{2,1,0:T(1,128)S(1)}, f32[54,1,128]{2,1,0:T(1,128)S(1)}, u32[]{:S(2)}, u32[]{:S(2)}) collective-permute-start(f32[54,1,128]{2,1,0:T(1,128)S(1)} %get-tuple-element.15), channel_id=1, source_target_pairs={{0,16},{16,32},{32,48},{48,64},{64,80},{80,96},{96,112},{112,128},... | collective-permute-start | bytes 82952 | tf_op jit(solution)/shard_map/ppermute | solution.py:22
  18.8 1.2 %fusion.130 = (f32[54,8,1]{2,1,0:T(8,128)S(1)}, f32[54,8,1]{2,1,0:T(8,128)S(1)}) fusion(f32[54,8,128]{2,1,0:T(8,128)} %param.11), kind=kLoop, calls=%fused_computation.223 | loop fusion | bytes 6912 | tf_op jit(solution)/shard_map/slice | solution.py:19
  20.0 0.7 copy-done.6
  21.8 4.3 %scatter_custom_fusion = s32[385]{0:T(512)S(1)} fusion(s32[1024]{0:T(1024)S(1)} %bitcast.94, s32[1024]{0:T(1024)S(1)} %iota.7, s32[]{:T(128)} %constant.12.clone.1), kind=kCustom, calls=%fused_computation.209 | custom fusion | bytes 1544 | tf_op jit(solution)/shard_map/scatter | solution.py:137
  26.1 0.7 compare_select_fusion.1
  26.8 0.7 copy-done.7
  27.7 5.8 %collective-permute-start.5 = (f32[54,1,128]{2,1,0:T(1,128)S(1)}, f32[54,1,128]{2,1,0:T(1,128)S(1)}, u32[]{:S(2)}, u32[]{:S(2)}) collective-permute-start(f32[54,1,128]{2,1,0:T(1,128)S(1)} %get-tuple-element.16), channel_id=1, source_target_pairs={{16,0},{32,16},{48,32},{64,48},{80,64},{96,80},{112,96},{128,112},... | collective-permute-start | bytes 82952 | tf_op jit(solution)/shard_map/ppermute | solution.py:23
  33.5 2.9 %collective-permute-start.6 = (f32[54,8,1]{2,1,0:T(8,128)S(1)}, f32[54,8,1]{2,1,0:T(8,128)S(1)}, u32[]{:S(2)}, u32[]{:S(2)}) collective-permute-start(f32[54,8,1]{2,1,0:T(8,128)S(1)} %get-tuple-element.14), channel_id=1, source_target_pairs={{1,0},{2,1},{3,2},{4,3},{5,4},{6,5},{7,6},{8,7},{9,8},{10,9},{11,1... | collective-permute-start | bytes 5192 | tf_op jit(solution)/shard_map/ppermute | solution.py:23
  36.4 2.9 %collective-permute-start.7 = (f32[54,8,1]{2,1,0:T(8,128)S(1)}, f32[54,8,1]{2,1,0:T(8,128)S(1)}, u32[]{:S(2)}, u32[]{:S(2)}) collective-permute-start(f32[54,8,1]{2,1,0:T(8,128)S(1)} %get-tuple-element.13), channel_id=1, source_target_pairs={{0,1},{1,2},{2,3},{3,4},{4,5},{5,6},{6,7},{7,8},{8,9},{9,10},{10,1... | collective-permute-start | bytes 5192 | tf_op jit(solution)/shard_map/ppermute | solution.py:22
  40.0 1.4 %collective-permute-done.6 = f32[54,8,1]{2,1,0:T(8,128)S(1)} collective-permute-done((f32[54,8,1]{2,1,0:T(8,128)S(1)}, f32[54,8,1]{2,1,0:T(8,128)S(1)}, u32[]{:S(2)}, u32[]{:S(2)}) %collective-permute-start.6) | collective-permute-done | bytes 1760 | tf_op jit(solution)/shard_map/ppermute | solution.py:23
  41.3 4.1 %collective-permute-done.7 = f32[54,8,1]{2,1,0:T(8,128)S(1)} collective-permute-done((f32[54,8,1]{2,1,0:T(8,128)S(1)}, f32[54,8,1]{2,1,0:T(8,128)S(1)}, u32[]{:S(2)}, u32[]{:S(2)}) %collective-permute-start.7) | collective-permute-done | bytes 1760 | tf_op jit(solution)/shard_map/ppermute | solution.py:22
  46.0 1.9 %collective-permute-start.8 = (f32[54,1,128]{2,1,0:T(1,128)S(1)}, f32[54,1,128]{2,1,0:T(1,128)S(1)}, u32[]{:S(2)}, u32[]{:S(2)}) collective-permute-start(f32[54,1,128]{2,1,0:T(1,128)S(1)} %get-tuple-element.11), channel_id=1, source_target_pairs={{0,16},{16,32},{32,48},{48,64},{64,80},{80,96},{96,112},{112,128},... | collective-permute-start | bytes 82952 | tf_op jit(solution)/shard_map/ppermute | solution.py:22
  47.9 5.8 %collective-permute-start.9 = (f32[54,1,128]{2,1,0:T(1,128)S(1)}, f32[54,1,128]{2,1,0:T(1,128)S(1)}, u32[]{:S(2)}, u32[]{:S(2)}) collective-permute-start(f32[54,1,128]{2,1,0:T(1,128)S(1)} %get-tuple-element.12), channel_id=1, source_target_pairs={{16,0},{32,16},{48,32},{64,48},{80,64},{96,80},{112,96},{128,112},... | collective-permute-start | bytes 82952 | tf_op jit(solution)/shard_map/ppermute | solution.py:23
  53.8 1.9 %collective-permute-start.10 = (f32[54,8,1]{2,1,0:T(8,128)S(1)}, f32[54,8,1]{2,1,0:T(8,128)S(1)}, u32[]{:S(2)}, u32[]{:S(2)}) collective-permute-start(f32[54,8,1]{2,1,0:T(8,128)S(1)} %get-tuple-element.10), channel_id=1, source_target_pairs={{1,0},{2,1},{3,2},{4,3},{5,4},{6,5},{7,6},{8,7},{9,8},{10,9},{11,1... | collective-permute-start | bytes 5192 | tf_op jit(solution)/shard_map/ppermute | solution.py:23
  55.7 3.9 %collective-permute-start.11 = (f32[54,8,1]{2,1,0:T(8,128)S(1)}, f32[54,8,1]{2,1,0:T(8,128)S(1)}, u32[]{:S(2)}, u32[]{:S(2)}) collective-permute-start(f32[54,8,1]{2,1,0:T(8,128)S(1)} %get-tuple-element.9), channel_id=1, source_target_pairs={{0,1},{1,2},{2,3},{3,4},{4,5},{5,6},{6,7},{7,8},{8,9},{9,10},{10,1... | collective-permute-start | bytes 5192 | tf_op jit(solution)/shard_map/ppermute | solution.py:22
  59.8 1.8 %collective-permute-done.10 = f32[54,8,1]{2,1,0:T(8,128)S(1)} collective-permute-done((f32[54,8,1]{2,1,0:T(8,128)S(1)}, f32[54,8,1]{2,1,0:T(8,128)S(1)}, u32[]{:S(2)}, u32[]{:S(2)}) %collective-permute-start.10) | collective-permute-done | bytes 1760 | tf_op jit(solution)/shard_map/ppermute | solution.py:23
  61.6 3.1 %collective-permute-done.11 = f32[54,8,1]{2,1,0:T(8,128)S(1)} collective-permute-done((f32[54,8,1]{2,1,0:T(8,128)S(1)}, f32[54,8,1]{2,1,0:T(8,128)S(1)}, u32[]{:S(2)}, u32[]{:S(2)}) %collective-permute-start.11) | collective-permute-done | bytes 1760 | tf_op jit(solution)/shard_map/ppermute | solution.py:22
  65.2 1.9 %collective-permute-start.12 = (f32[54,1,128]{2,1,0:T(1,128)S(1)}, f32[54,1,128]{2,1,0:T(1,128)S(1)}, u32[]{:S(2)}, u32[]{:S(2)}) collective-permute-start(f32[54,1,128]{2,1,0:T(1,128)S(1)} %get-tuple-element.7), channel_id=1, source_target_pairs={{0,16},{16,32},{32,48},{48,64},{64,80},{80,96},{96,112},{112,128},... | collective-permute-start | bytes 82952 | tf_op jit(solution)/shard_map/ppermute | solution.py:22
  67.2 5.8 %collective-permute-start.13 = (f32[54,1,128]{2,1,0:T(1,128)S(1)}, f32[54,1,128]{2,1,0:T(1,128)S(1)}, u32[]{:S(2)}, u32[]{:S(2)}) collective-permute-start(f32[54,1,128]{2,1,0:T(1,128)S(1)} %get-tuple-element.8), channel_id=1, source_target_pairs={{16,0},{32,16},{48,32},{64,48},{80,64},{96,80},{112,96},{128,112},... | collective-permute-start | bytes 82952 | tf_op jit(solution)/shard_map/ppermute | solution.py:23
  73.0 1.9 %collective-permute-start.14 = (f32[54,8,1]{2,1,0:T(8,128)S(1)}, f32[54,8,1]{2,1,0:T(8,128)S(1)}, u32[]{:S(2)}, u32[]{:S(2)}) collective-permute-start(f32[54,8,1]{2,1,0:T(8,128)S(1)} %get-tuple-element.6), channel_id=1, source_target_pairs={{1,0},{2,1},{3,2},{4,3},{5,4},{6,5},{7,6},{8,7},{9,8},{10,9},{11,1... | collective-permute-start | bytes 5192 | tf_op jit(solution)/shard_map/ppermute | solution.py:23
  75.0 3.9 %collective-permute-start.15 = (f32[54,8,1]{2,1,0:T(8,128)S(1)}, f32[54,8,1]{2,1,0:T(8,128)S(1)}, u32[]{:S(2)}, u32[]{:S(2)}) collective-permute-start(f32[54,8,1]{2,1,0:T(8,128)S(1)} %get-tuple-element.5), channel_id=1, source_target_pairs={{0,1},{1,2},{2,3},{3,4},{4,5},{5,6},{6,7},{7,8},{8,9},{9,10},{10,1... | collective-permute-start | bytes 5192 | tf_op jit(solution)/shard_map/ppermute | solution.py:22
  79.1 1.8 %collective-permute-done.14 = f32[54,8,1]{2,1,0:T(8,128)S(1)} collective-permute-done((f32[54,8,1]{2,1,0:T(8,128)S(1)}, f32[54,8,1]{2,1,0:T(8,128)S(1)}, u32[]{:S(2)}, u32[]{:S(2)}) %collective-permute-start.14) | collective-permute-done | bytes 1760 | tf_op jit(solution)/shard_map/ppermute | solution.py:23
  80.9 3.1 %collective-permute-done.15 = f32[54,8,1]{2,1,0:T(8,128)S(1)} collective-permute-done((f32[54,8,1]{2,1,0:T(8,128)S(1)}, f32[54,8,1]{2,1,0:T(8,128)S(1)}, u32[]{:S(2)}, u32[]{:S(2)}) %collective-permute-start.15) | collective-permute-done | bytes 1760 | tf_op jit(solution)/shard_map/ppermute | solution.py:22
  84.9 1.1 %gather_fusion = f32[384,55]{1,0:T(8,128)S(1)} fusion(f32[55,1024]{0,1:T(8,128)S(1)} %pad_maximum_fusion, s32[1024]{0:T(1024)S(1)} %pad_clamp_fusion), kind=kCustom, calls=%fused_computation | custom fusion | bytes 170496 | tf_op jit(solution)/shard_map/gather | solution.py:141
  92.4 2.8 %scatter_custom_fusion.1 = f32[54,1025]{0,1:T(8,128)S(1)} fusion(s32[384]{0:T(512)S(1)} %get-tuple-element.31, f32[384,54]{1,0:T(8,128)S(1)} %copy.30, f32[]{:T(128)} %constant.10.clone.1), kind=kCustom, calls=%fused_computation.120 | custom fusion | flops 20736 | bytes 221404 | tf_op jit(solution)/shard_map/scatter-add | solution.py:156
  95.3 0.9 copy.31
  (81 shorter events, 10.6 us)
Async XLA Ops:
  0.0 86.2 %copy-start = (bf16[256,256]{1,0:T(8,128)(2,1)S(1)}, bf16[256,256]{1,0:T(8,128)(2,1)}, u32[]{:S(2)}) copy-start(bf16[256,256]{1,0:T(8,128)(2,1)} %param.18) | copy-start | bytes 393220
  0.0 7.9 %copy-start.3 = (f32[2,8,128]{2,1,0:T(8,128)S(1)}, f32[2,8,128]{2,1,0:T(8,128)}, u32[]{:S(2)}) copy-start(f32[2,8,128]{2,1,0:T(8,128)} %param.13) | copy-start | bytes 24580
  0.0 7.9 %copy-start.4 = (f32[8,128]{1,0:T(8,128)S(1)}, f32[8,128]{1,0:T(8,128)}, u32[]{:S(2)}) copy-start(f32[8,128]{1,0:T(8,128)} %param.12) | copy-start | bytes 12292
  0.9 26.8 %collective-permute-start = (f32[3,8,1]{2,1,0:T(8,128)S(1)}, f32[3,8,1]{2,1,0:T(8,128)S(1)}, u32[]{:S(2)}, u32[]{:S(2)}) collective-permute-start(f32[3,8,1]{2,1,0:T(8,128)S(1)} %get-tuple-element.26), channel_id=1, source_target_pairs={{0,1},{1,2},{2,3},{3,4},{4,5},{5,6},{6,7},{7,8},{8,9},{9,10},{10,1... | collective-permute-start | bytes 296 | tf_op jit(solution)/shard_map/ppermute | solution.py:22
  3.8 29.7 %collective-permute-start.3 = (f32[3,8,1]{2,1,0:T(8,128)S(1)}, f32[3,8,1]{2,1,0:T(8,128)S(1)}, u32[]{:S(2)}, u32[]{:S(2)}) collective-permute-start(f32[3,8,1]{2,1,0:T(8,128)S(1)} %get-tuple-element.27), channel_id=1, source_target_pairs={{1,0},{2,1},{3,2},{4,3},{5,4},{6,5},{7,6},{8,7},{9,8},{10,9},{11,1... | collective-permute-start | bytes 296 | tf_op jit(solution)/shard_map/ppermute | solution.py:23
  8.0 28.5 %collective-permute-start.1 = (f32[3,1,128]{2,1,0:T(1,128)S(1)}, f32[3,1,128]{2,1,0:T(1,128)S(1)}, u32[]{:S(2)}, u32[]{:S(2)}) collective-permute-start(f32[3,1,128]{2,1,0:T(1,128)S(1)} %get-tuple-element.24), channel_id=1, source_target_pairs={{0,16},{16,32},{32,48},{48,64},{64,80},{80,96},{96,112},{112,128},... | collective-permute-start | bytes 4616 | tf_op jit(solution)/shard_map/ppermute | solution.py:22
  9.9 29.5 %collective-permute-start.2 = (f32[3,1,128]{2,1,0:T(1,128)S(1)}, f32[3,1,128]{2,1,0:T(1,128)S(1)}, u32[]{:S(2)}, u32[]{:S(2)}) collective-permute-start(f32[3,1,128]{2,1,0:T(1,128)S(1)} %get-tuple-element.25), channel_id=1, source_target_pairs={{16,0},{32,16},{48,32},{64,48},{80,64},{96,80},{112,96},{128,112},... | collective-permute-start | bytes 4616 | tf_op jit(solution)/shard_map/ppermute | solution.py:23
  16.8 3.2 %copy-start.1 = (f32[54,8,128]{2,1,0:T(8,128)S(1)}, f32[54,8,128]{2,1,0:T(8,128)}, u32[]{:S(2)}) copy-start(f32[54,8,128]{2,1,0:T(8,128)} %param.11) | copy-start | bytes 663556
  16.8 23.0 %collective-permute-start.4 = (f32[54,1,128]{2,1,0:T(1,128)S(1)}, f32[54,1,128]{2,1,0:T(1,128)S(1)}, u32[]{:S(2)}, u32[]{:S(2)}) collective-permute-start(f32[54,1,128]{2,1,0:T(1,128)S(1)} %get-tuple-element.15), channel_id=1, source_target_pairs={{0,16},{16,32},{32,48},{48,64},{64,80},{80,96},{96,112},{112,128},... | collective-permute-start | bytes 82952 | tf_op jit(solution)/shard_map/ppermute | solution.py:22
  20.0 0.7 copy-start.6
  26.8 0.7 copy-start.7
  27.7 11.9 %collective-permute-start.5 = (f32[54,1,128]{2,1,0:T(1,128)S(1)}, f32[54,1,128]{2,1,0:T(1,128)S(1)}, u32[]{:S(2)}, u32[]{:S(2)}) collective-permute-start(f32[54,1,128]{2,1,0:T(1,128)S(1)} %get-tuple-element.16), channel_id=1, source_target_pairs={{16,0},{32,16},{48,32},{64,48},{80,64},{96,80},{112,96},{128,112},... | collective-permute-start | bytes 82952 | tf_op jit(solution)/shard_map/ppermute | solution.py:23
  33.5 7.8 %collective-permute-start.6 = (f32[54,8,1]{2,1,0:T(8,128)S(1)}, f32[54,8,1]{2,1,0:T(8,128)S(1)}, u32[]{:S(2)}, u32[]{:S(2)}) collective-permute-start(f32[54,8,1]{2,1,0:T(8,128)S(1)} %get-tuple-element.14), channel_id=1, source_target_pairs={{1,0},{2,1},{3,2},{4,3},{5,4},{6,5},{7,6},{8,7},{9,8},{10,9},{11,1... | collective-permute-start | bytes 5192 | tf_op jit(solution)/shard_map/ppermute | solution.py:23
  36.4 9.0 %collective-permute-start.7 = (f32[54,8,1]{2,1,0:T(8,128)S(1)}, f32[54,8,1]{2,1,0:T(8,128)S(1)}, u32[]{:S(2)}, u32[]{:S(2)}) collective-permute-start(f32[54,8,1]{2,1,0:T(8,128)S(1)} %get-tuple-element.13), channel_id=1, source_target_pairs={{0,1},{1,2},{2,3},{3,4},{4,5},{5,6},{6,7},{7,8},{8,9},{9,10},{10,1... | collective-permute-start | bytes 5192 | tf_op jit(solution)/shard_map/ppermute | solution.py:22
  46.0 13.7 %collective-permute-start.8 = (f32[54,1,128]{2,1,0:T(1,128)S(1)}, f32[54,1,128]{2,1,0:T(1,128)S(1)}, u32[]{:S(2)}, u32[]{:S(2)}) collective-permute-start(f32[54,1,128]{2,1,0:T(1,128)S(1)} %get-tuple-element.11), channel_id=1, source_target_pairs={{0,16},{16,32},{32,48},{48,64},{64,80},{80,96},{96,112},{112,128},... | collective-permute-start | bytes 82952 | tf_op jit(solution)/shard_map/ppermute | solution.py:22
  47.9 11.8 %collective-permute-start.9 = (f32[54,1,128]{2,1,0:T(1,128)S(1)}, f32[54,1,128]{2,1,0:T(1,128)S(1)}, u32[]{:S(2)}, u32[]{:S(2)}) collective-permute-start(f32[54,1,128]{2,1,0:T(1,128)S(1)} %get-tuple-element.12), channel_id=1, source_target_pairs={{16,0},{32,16},{48,32},{64,48},{80,64},{96,80},{112,96},{128,112},... | collective-permute-start | bytes 82952 | tf_op jit(solution)/shard_map/ppermute | solution.py:23
  53.8 7.8 %collective-permute-start.10 = (f32[54,8,1]{2,1,0:T(8,128)S(1)}, f32[54,8,1]{2,1,0:T(8,128)S(1)}, u32[]{:S(2)}, u32[]{:S(2)}) collective-permute-start(f32[54,8,1]{2,1,0:T(8,128)S(1)} %get-tuple-element.10), channel_id=1, source_target_pairs={{1,0},{2,1},{3,2},{4,3},{5,4},{6,5},{7,6},{8,7},{9,8},{10,9},{11,1... | collective-permute-start | bytes 5192 | tf_op jit(solution)/shard_map/ppermute | solution.py:23
  55.7 9.0 %collective-permute-start.11 = (f32[54,8,1]{2,1,0:T(8,128)S(1)}, f32[54,8,1]{2,1,0:T(8,128)S(1)}, u32[]{:S(2)}, u32[]{:S(2)}) collective-permute-start(f32[54,8,1]{2,1,0:T(8,128)S(1)} %get-tuple-element.9), channel_id=1, source_target_pairs={{0,1},{1,2},{2,3},{3,4},{4,5},{5,6},{6,7},{7,8},{8,9},{9,10},{10,1... | collective-permute-start | bytes 5192 | tf_op jit(solution)/shard_map/ppermute | solution.py:22
  65.2 13.7 %collective-permute-start.12 = (f32[54,1,128]{2,1,0:T(1,128)S(1)}, f32[54,1,128]{2,1,0:T(1,128)S(1)}, u32[]{:S(2)}, u32[]{:S(2)}) collective-permute-start(f32[54,1,128]{2,1,0:T(1,128)S(1)} %get-tuple-element.7), channel_id=1, source_target_pairs={{0,16},{16,32},{32,48},{48,64},{64,80},{80,96},{96,112},{112,128},... | collective-permute-start | bytes 82952 | tf_op jit(solution)/shard_map/ppermute | solution.py:22
  67.2 11.8 %collective-permute-start.13 = (f32[54,1,128]{2,1,0:T(1,128)S(1)}, f32[54,1,128]{2,1,0:T(1,128)S(1)}, u32[]{:S(2)}, u32[]{:S(2)}) collective-permute-start(f32[54,1,128]{2,1,0:T(1,128)S(1)} %get-tuple-element.8), channel_id=1, source_target_pairs={{16,0},{32,16},{48,32},{64,48},{80,64},{96,80},{112,96},{128,112},... | collective-permute-start | bytes 82952 | tf_op jit(solution)/shard_map/ppermute | solution.py:23
  73.0 7.8 %collective-permute-start.14 = (f32[54,8,1]{2,1,0:T(8,128)S(1)}, f32[54,8,1]{2,1,0:T(8,128)S(1)}, u32[]{:S(2)}, u32[]{:S(2)}) collective-permute-start(f32[54,8,1]{2,1,0:T(8,128)S(1)} %get-tuple-element.6), channel_id=1, source_target_pairs={{1,0},{2,1},{3,2},{4,3},{5,4},{6,5},{7,6},{8,7},{9,8},{10,9},{11,1... | collective-permute-start | bytes 5192 | tf_op jit(solution)/shard_map/ppermute | solution.py:23
  75.0 9.0 %collective-permute-start.15 = (f32[54,8,1]{2,1,0:T(8,128)S(1)}, f32[54,8,1]{2,1,0:T(8,128)S(1)}, u32[]{:S(2)}, u32[]{:S(2)}) collective-permute-start(f32[54,8,1]{2,1,0:T(8,128)S(1)} %get-tuple-element.5), channel_id=1, source_target_pairs={{0,1},{1,2},{2,3},{3,4},{4,5},{5,6},{6,7},{7,8},{8,9},{9,10},{10,1... | collective-permute-start | bytes 5192 | tf_op jit(solution)/shard_map/ppermute | solution.py:22
  86.0 0.8 copy-start.8
  86.2 0.7 copy-start.9
  86.2 0.7 copy-start.10
  86.9 0.7 copy-start.2
  86.9 0.7 copy-start.5
where the time goes:
time: 97.1 us; the launch traced here: 96.2 us
  starting transfers between devices  55.4 us (57%)
  waiting for transfers between devices  15.4 us (16%)
  local copies, waits for them, and re-layouts  12.3 us (13%)
  other arithmetic  7.6 us (8%)
  matrix products  4.9 us (5%)
    ppermute x8, starting transfers between devices, padded_2(): lax.ppermute(initial, axis, [(b, a) for a, b in up])  33.9 us
    ppermute x8, starting transfers between devices, padded_2(): lax.ppermute(last, axis, up)  21.5 us
    ppermute x8, waiting for transfers between devices, padded_2(): lax.ppermute(last, axis, up)  10.4 us
    ppermute x8, waiting for transfers between devices, padded_2(): lax.ppermute(initial, axis, [(b, a) for a, b in up])  4.97 us
    scatter x1, local copies, waits for them, and re-layouts, shards(): slot_cell = jnp.zeros((cell_capacity + 1,), jnp.int32).at[jnp.where(activ...  4.3 us
    dot_general x8, matrix products, network(): jnp.dot(hidden_level_matrix, hidden, preferred_element_type=jnp.float32)  3.28 us
    scatter-add x1, other arithmetic, shards(): increments = jnp.zeros((species_count, cell_total + 1), jnp.float32).at[:...  2.84 us
    slice x6, local copies, waits for them, and re-layouts, padded_2(): last = lax.slice_in_dim(array, length - width, length, axis=dim)  2.55 us
  transfers between devices with their start and end apart: 16, of which 6 were waited for; matrix products, arithmetic and copies ran while one was open for 10% of the time, Pallas kernels for 0%

commit v1 on v0

v1 whole, which is shorter than its diff:
```python
import functools

import jax
import jax.numpy as jnp
from jax import lax
from jax.experimental import pallas as pl
from jax.experimental.pallas import tpu as pltpu
from jax.sharding import PartitionSpec as P

SUBSTEPS = 8
STEPS = 3
KINDS = 54
HID = 256
ROWS = 8
LANES = 128
CAP = 384
CHUNK = 128
CHANNELS = 64
DIFF, SPEED_C, SPEED_R, INSIDE = 54, 55, 56, 57
WIDE = 10
chem_step = 0.0625
f32 = jnp.float32
bf16 = jnp.bfloat16


def iota(shape, axis):
    return lax.broadcasted_iota(jnp.int32, shape, axis)


def planes_kernel(y_ref, d_ref, v_ref, all_ref, top_ref, bottom_ref):
    for r in range(ROWS):
        refs = [all_ref.at[r]]
        if r < STEPS:
            refs.append(top_ref.at[r])
        if r >= ROWS - STEPS:
            refs.append(bottom_ref.at[r - ROWS + STEPS])
        species = y_ref[:, r, :]
        for ref in refs:
            ref[0:KINDS, :] = species
            ref[DIFF : DIFF + 1, :] = d_ref[r : r + 1, :]
            ref[SPEED_C : SPEED_C + 1, :] = v_ref[0, r : r + 1, :]
            ref[SPEED_R : SPEED_R + 1, :] = v_ref[1, r : r + 1, :]
            ref[INSIDE:CHANNELS, :] = jnp.ones((CHANNELS - INSIDE, LANES), f32)


def strip_kernel(all_ref, low_ref, high_ref, strip_ref):
    lane = iota((CHANNELS, LANES), 1)
    total = jnp.zeros((CHANNELS, LANES), f32)
    for j in range(ROWS + 4):
        row = j - 2
        if row < 0:
            plane = low_ref[STEPS + row]
        elif row < ROWS:
            plane = all_ref[row]
        else:
            plane = high_ref[row - ROWS]
        at = WIDE * j
        first = pltpu.roll(plane, (at + 3) % LANES, 1)
        second = pltpu.roll(plane, (at + 7) % LANES, 1)
        total = jnp.where((lane >= at) & (lane < at + 5), first, total)
        total = jnp.where((lane >= at + 5) & (lane < at + WIDE), second, total)
    strip_ref[...] = total


def prepare_kernel(act_ref, w1_ref, w2_ref, w3_ref, b3_ref, pick_ref, w1t_ref, w2t_ref, mix_ref, w3t_ref, bias_ref):
    act = act_ref[...].astype(f32)
    before = (iota((LANES, LANES), 0) < iota((LANES, LANES), 1)).astype(f32).astype(bf16)
    inner = jnp.dot(act.astype(bf16), before, preferred_element_type=f32)
    counts = jnp.broadcast_to(jnp.sum(act, axis=1, keepdims=True), (ROWS, LANES))
    row = iota((ROWS, LANES), 0)
    outer = jnp.zeros((ROWS, LANES), f32)
    for k in range(ROWS - 1):
        outer = outer + jnp.where(row > k, jnp.broadcast_to(counts[k : k + 1, :], (ROWS, LANES)), 0.0)
    slot = jnp.where(act > 0.0, inner + outer, -1.0).astype(jnp.int32)
    slots = iota((CAP, LANES), 0)
    for r in range(ROWS):
        hit = slots == jnp.broadcast_to(slot[r : r + 1, :], (CAP, LANES))
        pick_ref[:, r * LANES : (r + 1) * LANES] = jnp.where(hit, 1.0, 0.0).astype(bf16)
    w1t = w1_ref[...].astype(f32).T
    w1t_ref[...] = jnp.zeros((2 * CHANNELS, HID), bf16)
    for k in range(2):
        w1t_ref[k * CHANNELS : k * CHANNELS + KINDS + 1, :] = w1t.astype(bf16)
    w2t_ref[...] = w2_ref[...].astype(f32).T.astype(bf16)
    w3t = w3_ref[...].astype(f32).T
    w3t_ref[...] = w3t.astype(bf16)
    part = w1t[0:KINDS, :]
    mix = jnp.dot(w3t.astype(bf16), part.astype(bf16), preferred_element_type=f32)
    mix_ref[...] = (chem_step * mix).astype(bf16)
    bias_ref[...] = chem_step * jnp.sum(part * b3_ref[...], axis=0, keepdims=True)


def face(d_low, d_high, u_low, u_high):
    d = 0.5 * (d_low + d_high)
    u = 0.5 * (u_low + u_high)
    return d - jnp.minimum(u, 0.0), d + jnp.maximum(u, 0.0)


def main_kernel(
    all_ref, low_ref, high_ref, own_ref, left_ref, right_ref, heat_ref,
    pick_ref, w1t_ref, w2t_ref, mix_ref, w3t_ref, bias_ref, b1_ref, b2_ref, b3_ref,
    out_ref, base_ref, coef_ref, one_ref, two_ref, feat_ref, pre_ref, sum_ref,
):
    lane = iota((CHANNELS, LANES), 1)
    place = lane % WIDE
    strip = jnp.where(place < 3, left_ref[...], jnp.where(place < 7, own_ref[...], right_ref[...]))
    lane1 = iota((1, LANES), 1)
    ds, us, vs, inside = (strip[k : k + 1, :] for k in (DIFF, SPEED_C, SPEED_R, INSIDE))
    inside = jnp.where(lane1 < WIDE * (ROWS + 4), inside, 0.0)
    ahead, behind = LANES - 1, 1
    a_r, b_r = face(ds, pltpu.roll(ds, ahead, 1), us, pltpu.roll(us, ahead, 1))
    a_l, b_l = pltpu.roll(a_r, behind, 1), pltpu.roll(b_r, behind, 1)
    a_u, b_u = face(ds, pltpu.roll(ds, LANES - WIDE, 1), vs, pltpu.roll(vs, LANES - WIDE, 1))
    a_d, b_d = pltpu.roll(a_u, WIDE, 1), pltpu.roll(b_u, WIDE, 1)
    strip_coef = [
        jnp.broadcast_to(inside * c, (56, LANES)) for c in (1.0 - b_r - a_l - b_u - a_d, a_r, b_l, a_u, b_d)
    ]
    for k in range(4):
        for i in range(STEPS):
            base_ref[k, 8 + i : 9 + i, :] = low_ref[i, DIFF + k : DIFF + k + 1, :]
            base_ref[k, 19 + i : 20 + i, :] = high_ref[i, DIFF + k : DIFF + k + 1, :]
        base_ref[k, 0:8, :] = jnp.zeros((8, LANES), f32)
        base_ref[k, 22:32, :] = jnp.zeros((10, LANES), f32)
        for r in range(ROWS):
            base_ref[k, 11 + r : 12 + r, :] = all_ref[r, DIFF + k : DIFF + k + 1, :]
    here, up, down = (lambda k: base_ref[k, 8:24, :]), (lambda k: base_ref[k, 9:25, :]), (lambda k: base_ref[k, 7:23, :])
    lane16, row16 = iota((16, LANES), 1), iota((16, LANES), 0)

    def column(values, c):
        hit = lane16 == WIDE * (row16 - 1) + c
        return jnp.sum(jnp.where(hit, jnp.broadcast_to(values, (16, LANES)), 0.0), axis=1, keepdims=True)

    d, u, v, ins = here(0), here(1), here(2), here(3)
    after = lambda x, s: jnp.where(lane16 == LANES - 1, column(s, 7), pltpu.roll(x, ahead, 1))
    prior = lambda x, s: jnp.where(lane16 == 0, column(s, 2), pltpu.roll(x, behind, 1))
    a_r, b_r = face(d, after(d, ds), u, after(u, us))
    a_l, b_l = face(prior(d, ds), d, prior(u, us), u)
    a_u, b_u = face(d, up(0), v, up(2))
    a_d, b_d = face(down(0), d, down(2), v)
    for k, c in enumerate((1.0 - b_r - a_l - b_u - a_d, a_r, b_l, a_u, b_d)):
        coef_ref[k] = ins * c

    def load(step, i):
        if step == 0:
            if i < STEPS:
                return low_ref[i, 0:56, :]
            if i < STEPS + ROWS:
                return all_ref[i - STEPS, 0:56, :]
            return high_ref[i - STEPS - ROWS, 0:56, :]
        return (one_ref if step % 2 else two_ref)[i]

    edge = iota((56, LANES), 1)
    strip = strip[0:56, :]
    for step in range(STEPS):
        target = two_ref if step % 2 else one_ref
        for i in range(1 + step, 13 - step):
            mine = load(step, i)
            at = WIDE * (i - 1)
            after_v = jnp.where(edge == LANES - 1, pltpu.roll(strip, (2 * LANES - 8 - at) % LANES, 1), pltpu.roll(mine, ahead, 1))
            prior_v = jnp.where(edge == 0, pltpu.roll(strip, (2 * LANES - 2 - at) % LANES, 1), pltpu.roll(mine, behind, 1))
            c = [jnp.broadcast_to(coef_ref[k, i : i + 1, :], (56, LANES)) for k in range(5)]
            target[i] = (
                c[0] * mine + c[1] * after_v + c[2] * prior_v + c[3] * load(step, i + 1) + c[4] * load(step, i - 1)
            )
        if step < STEPS - 1:
            strip = (
                strip_coef[0] * strip
                + strip_coef[1] * pltpu.roll(strip, ahead, 1)
                + strip_coef[2] * pltpu.roll(strip, behind, 1)
                + strip_coef[3] * pltpu.roll(strip, LANES - WIDE, 1)
                + strip_coef[4] * pltpu.roll(strip, WIDE, 1)
            )
    moved = one_ref if STEPS % 2 else two_ref

    sub = iota((56, LANES), 0)
    for r in range(ROWS):
        block = jnp.where(sub < KINDS, moved[r + STEPS], 0.0)
        block = jnp.where(sub == KINDS, jnp.broadcast_to(heat_ref[r : r + 1, :], (56, LANES)), block)
        block = jnp.concatenate([block, jnp.zeros((8, LANES), f32)], 0)
        coarse = block.astype(bf16)
        fine = jnp.where(iota((CHANNELS, LANES), 0) < KINDS, block - coarse.astype(f32), 0.0).astype(bf16)
        feat_ref[0:CHANNELS, r * LANES : (r + 1) * LANES] = coarse
        feat_ref[CHANNELS:, r * LANES : (r + 1) * LANES] = fine
    slots = lax.dot_general(pick_ref[...], feat_ref[...], (((1,), (1,)), ((), ())), preferred_element_type=f32)
    for k in range(CAP // CHUNK):
        s = slice(k * CHUNK, (k + 1) * CHUNK)
        pre_ref[s, :] = jnp.dot(slots[s, :].astype(bf16), w1t_ref[...], preferred_element_type=f32) + b1_ref[...]
    for index in range(SUBSTEPS):
        for k in range(CAP // CHUNK):
            s = slice(k * CHUNK, (k + 1) * CHUNK)
            first = jnp.tanh(pre_ref[s, :]).astype(bf16)
            second = jnp.dot(first, w2t_ref[...], preferred_element_type=f32) + b2_ref[...]
            second = jnp.tanh(second).astype(bf16)
            wide = second.astype(f32)
            sum_ref[s, :] = wide if index == 0 else sum_ref[s, :] + wide
            if index < SUBSTEPS - 1:
                pre_ref[s, :] += jnp.dot(second, mix_ref[...], preferred_element_type=f32) + bias_ref[...]
    total = sum_ref[...]
    high = total.astype(bf16)
    low = (total - high.astype(f32)).astype(bf16)
    rate = jnp.dot(high, w3t_ref[...], preferred_element_type=f32) + jnp.dot(low, w3t_ref[...], preferred_element_type=f32)
    rate = chem_step * (rate + SUBSTEPS * b3_ref[...])
    rate = jnp.concatenate([rate, jnp.zeros((CAP, LANES - KINDS), f32)], 1).T[0:56, :]
    high = rate.astype(bf16)
    low = (rate - high.astype(f32)).astype(bf16)
    for r in range(ROWS):
        block = pick_ref[:, r * LANES : (r + 1) * LANES]
        gain = jnp.dot(high, block, preferred_element_type=f32) + jnp.dot(low, block, preferred_element_type=f32)
        out_ref[:, r, :] = (moved[r + STEPS] + gain)[0:KINDS, :]


def vmem(count):
    return [pl.BlockSpec(memory_space=pltpu.VMEM)] * count


def call(kernel, shapes, operands, name, scratch=(), cost=None):
    return pl.pallas_call(
        kernel,
        out_shape=[jax.ShapeDtypeStruct(s, t) for s, t in shapes],
        in_specs=vmem(len(operands)),
        out_specs=vmem(len(shapes)),
        scratch_shapes=[pltpu.VMEM(s, t) for s, t in scratch],
        compiler_params=pltpu.CompilerParams(vmem_limit_bytes=16 << 20),
        cost_estimate=cost,
        name=name,
    )(*operands)


def shift(low_sends, high_sends, axis):
    devices = lax.axis_size(axis)
    up = [(i, i + 1) for i in range(devices - 1)]
    return lax.ppermute(low_sends, axis, up), lax.ppermute(high_sends, axis, [(b, a) for a, b in up])


def shards(y, d, v, heat, active, w1, b1, w2, b2, w3, b3):
    plane = (CHANNELS, LANES)
    every, top, bottom = call(
        planes_kernel, [((ROWS,) + plane, f32), ((STEPS,) + plane, f32), ((STEPS,) + plane, f32)], (y, d, v), "planes"
    )
    low, high = shift(bottom, top, "row")
    (strip,) = call(strip_kernel, [(plane, f32)], (every, low, high), "strip")
    left, right = shift(strip, strip, "col")
    picks = call(
        prepare_kernel,
        [((CAP, ROWS * LANES), bf16), ((2 * CHANNELS, HID), bf16), ((HID, HID), bf16), ((HID, HID), bf16), ((HID, KINDS), bf16), ((1, HID), f32)],
        (active, w1, w2, w3, b3[:, None]),
        "prepare",
        cost=pl.CostEstimate(flops=20_000_000, bytes_accessed=2_000_000, transcendentals=0),
    )
    (out,) = call(
        main_kernel,
        [((KINDS, ROWS, LANES), f32)],
        (every, low, high, strip, left, right, heat, *picks, b1[None], b2[None], b3[None]),
        "main",
        scratch=[
            ((4, 32, LANES), f32), ((5, 16, LANES), f32), ((14, 56, LANES), f32), ((14, 56, LANES), f32),
            ((2 * CHANNELS, ROWS * LANES), bf16), ((CAP, HID), f32), ((CAP, HID), f32),
        ],
    )
    return out


def solution(mesh):
    tile, rest = P("row", "col"), P()
    stack = P(None, "row", "col")
    in_specs = (stack, tile, stack, tile, tile, rest, rest, rest, rest, rest, rest)
    return jax.shard_map(shards, mesh=mesh, in_specs=in_specs, out_specs=stack, check_vma=False)
```

time: 97.1 us -> 30 us (0.31)
  the two profiles are of different devices: /device:TPU:386 before, /device:TPU:409 now
where the time goes in v1:
time: 30 us; the launch traced here: 29.6 us
  starting transfers between devices  11 us (37%)
  waiting for transfers between devices  8.56 us (29%)
  Pallas kernels  6.06 us (20%)
  local copies, waits for them, and re-layouts  3.89 us (13%)
    ppermute x2, waiting for transfers between devices, shift(): lax.ppermute(high_sends, axis, [(b, a) for a, b in up])  6.11 us
    pallas_call x4, Pallas kernels, call(): pl.pallas_call(kernel, out_shape=[jax.ShapeDtypeStruct(s, t) for s, t in...  6.06 us
    ppermute x2, starting transfers between devices, shift(): lax.ppermute(high_sends, axis, [(b, a) for a, b in up])  5.77 us
    ppermute x2, starting transfers between devices, shift(): lax.ppermute(low_sends, axis, up)  5.26 us
    unnamed x23, local copies, waits for them, and re-layouts  3.78 us
    ppermute x2, waiting for transfers between devices, shift(): lax.ppermute(low_sends, axis, up)  2.45 us
  transfers between devices with their start and end apart: 4, of which 2 were waited for; matrix products, arithmetic and copies ran while one was open for 1% of the time, Pallas kernels for 2%

profile of v1, /device:TPU:409, one launch (start us, length us, event | category | flops | bytes accessed | tf_op | source)
XLA Modules:
  0.0 29.6 jit_solution(441877106510905517)
XLA Ops:
  0.0 0.0 copy-start
  0.0 0.9 %copy-done = f32[54,8,128]{2,1,0:T(8,128)S(1)} copy-done((f32[54,8,128]{2,1,0:T(8,128)S(1)}, f32[54,8,128]{2,1,0:T(8,128)}, u32[]{:S(2)}) %copy-start) | copy-done | bytes 221208
  0.9 0.0 copy-start.3
  0.9 0.7 %copy-done.3 = f32[2,8,128]{2,1,0:T(8,128)S(1)} copy-done((f32[2,8,128]{2,1,0:T(8,128)S(1)}, f32[2,8,128]{2,1,0:T(8,128)}, u32[]{:S(2)}) %copy-start.3) | copy-done | bytes 8216
  1.6 0.0 copy-start.4
  1.6 0.7 %copy-done.4 = f32[8,128]{1,0:T(8,128)S(1)} copy-done((f32[8,128]{1,0:T(8,128)S(1)}, f32[8,128]{1,0:T(8,128)}, u32[]{:S(2)}) %copy-start.4) | copy-done | bytes 4120
  2.3 0.1 planes.1
  2.5 3.3 %collective-permute-start = (f32[3,64,128]{2,1,0:T(8,128)S(1)}, f32[3,64,128]{2,1,0:T(8,128)S(1)}, u32[]{:S(2)}, u32[]{:S(2)}) collective-permute-start(f32[3,64,128]{2,1,0:T(8,128)S(1)} %get-tuple-element.15), channel_id=1, source_target_pairs={{0,16},{16,32},{32,48},{48,64},{64,80},{80,96},{96,112},{112,128},... | collective-permute-start | bytes 294920 | tf_op jit(solution)/shard_map/ppermute | solution.py:231
  5.8 1.9 %collective-permute-start.1 = (f32[3,64,128]{2,1,0:T(8,128)S(1)}, f32[3,64,128]{2,1,0:T(8,128)S(1)}, u32[]{:S(2)}, u32[]{:S(2)}) collective-permute-start(f32[3,64,128]{2,1,0:T(8,128)S(1)} %get-tuple-element.16), channel_id=1, source_target_pairs={{16,0},{32,16},{48,32},{64,48},{80,64},{96,80},{112,96},{128,112},... | collective-permute-start | bytes 294920 | tf_op jit(solution)/shard_map/ppermute | solution.py:231
  7.7 0.0 collective-permute-done.low_ref
  7.8 6.1 %collective-permute-done.1.high_ref = f32[3,64,128]{2,1,0:T(8,128)S(1)} collective-permute-done((f32[3,64,128]{2,1,0:T(8,128)S(1)}, f32[3,64,128]{2,1,0:T(8,128)S(1)}, u32[]{:S(2)}, u32[]{:S(2)}) %collective-permute-start.1) | collective-permute-done | bytes 98336 | tf_op jit(solution)/shard_map/ppermute | solution.py:231
  13.9 0.0 copy-start.1
  13.9 0.3 strip.1.own_ref
  14.1 0.0 copy-start.7
  14.1 0.0 copy-start.10
  14.2 3.8 %collective-permute-start.3 = (f32[64,128]{1,0:T(8,128)S(1)}, f32[64,128]{1,0:T(8,128)S(1)}, u32[]{:S(2)}, u32[]{:S(2)}) collective-permute-start(f32[64,128]{1,0:T(8,128)S(1)} %strip.1.own_ref), channel_id=1, source_target_pairs={{1,0},{2,1},{3,2},{4,3},{5,4},{6,5},{7,6},{8,7},{9,8},{10,9},{11,1... | collective-permute-start | bytes 98312 | tf_op jit(solution)/shard_map/ppermute | solution.py:231
  18.0 1.9 %collective-permute-start.2 = (f32[64,128]{1,0:T(8,128)S(1)}, f32[64,128]{1,0:T(8,128)S(1)}, u32[]{:S(2)}, u32[]{:S(2)}) collective-permute-start(f32[64,128]{1,0:T(8,128)S(1)} %strip.1.own_ref), channel_id=1, source_target_pairs={{0,1},{1,2},{2,3},{3,4},{4,5},{5,6},{6,7},{7,8},{8,9},{9,10},{10,1... | collective-permute-start | bytes 98312 | tf_op jit(solution)/shard_map/ppermute | solution.py:231
  19.9 0.0 copy-done.7
  19.9 0.1 copy.13.b3_ref
  20.1 0.0 copy-done.10
  20.1 0.0 copy-start.5
  20.1 0.1 copy.12.w1_ref
  20.2 0.0 copy-done.1
  20.2 0.6 %copy-done.2 = bf16[54,256]{1,0:T(8,128)(2,1)S(1)} copy-done((bf16[54,256]{1,0:T(8,128)(2,1)S(1)}, bf16[54,256]{1,0:T(8,128)(2,1)}, u32[]{:S(2)}) %copy-start.2) | copy-done | bytes 27672
  20.8 0.0 copy-done.5
  20.8 0.6 %prepare.1 = (bf16[384,1024]{1,0:T(8,128)(2,1)S(1)}, bf16[128,256]{1,0:T(8,128)(2,1)S(1)}, bf16[256,256]{1,0:T(8,128)(2,1)S(1)}, bf16[256,256]{1,0:T(8,128)(2,1)...) custom-call(s32[8,128]{1,0:T(8,128)S(1)} %copy-done.5, bf16[256,55]{1,0:T(8,128)(2,1)S(1)} %copy.12.w1_ref, ...), custom_call_target="tpu_custom_call" | custom-call | flops 20000000 | bytes 2000000 | tf_op jit(solution)/shard_map/prepare/pallas_call | solution.py:216
  21.4 0.0 collective-permute-done.3.right_ref
  21.4 2.5 %collective-permute-done.2.left_ref = f32[64,128]{1,0:T(8,128)S(1)} collective-permute-done((f32[64,128]{1,0:T(8,128)S(1)}, f32[64,128]{1,0:T(8,128)S(1)}, u32[]{:S(2)}, u32[]{:S(2)}) %collective-permute-start.2) | collective-permute-done | bytes 32800 | tf_op jit(solution)/shard_map/ppermute | solution.py:231
  23.9 0.7 %copy-done.9 = f32[256]{0:T(256)S(1)} copy-done((f32[256]{0:T(256)S(1)}, f32[256]{0:T(256)}, u32[]{:S(2)}) %copy-start.9) | copy-done | bytes 1048
  24.6 0.0 copy-done.6
  24.6 0.0 copy-done.8
  24.6 5.1 %main.1 = f32[54,8,128]{2,1,0:T(8,128)} custom-call(f32[8,64,128]{2,1,0:T(8,128)S(1)} %get-tuple-element.14.all_ref, f32[3,64,128]{2,1,0:T(8,128)S(1)} %collective-permute-done.low_ref, f32[3,64,128]{2,1,0:T(8,128)S(1)} %collective-permute-done.1.high_ref, f32[64,128]{1,0:T(8,128)S(1)} %strip.1.own_ref, f32[64,128]{1,0:T(8,128)S(1)} %collective-permute-done.2.left_ref, ...), custom_call_target="tpu_custom_call" | custom-call | tf_op jit(solution)/shard_map/main/pallas_call | solution.py:216
  (4 shorter events, 0.0 us)
Async XLA Ops:
  0.0 0.9 %copy-start = (f32[54,8,128]{2,1,0:T(8,128)S(1)}, f32[54,8,128]{2,1,0:T(8,128)}, u32[]{:S(2)}) copy-start(f32[54,8,128]{2,1,0:T(8,128)} %y_ref.1) | copy-start | bytes 663556
  0.9 0.7 %copy-start.3 = (f32[2,8,128]{2,1,0:T(8,128)S(1)}, f32[2,8,128]{2,1,0:T(8,128)}, u32[]{:S(2)}) copy-start(f32[2,8,128]{2,1,0:T(8,128)} %v_ref.1) | copy-start | bytes 24580
  1.6 0.7 %copy-start.4 = (f32[8,128]{1,0:T(8,128)S(1)}, f32[8,128]{1,0:T(8,128)}, u32[]{:S(2)}) copy-start(f32[8,128]{1,0:T(8,128)} %d_ref.1) | copy-start | bytes 12292
  2.5 5.3 %collective-permute-start = (f32[3,64,128]{2,1,0:T(8,128)S(1)}, f32[3,64,128]{2,1,0:T(8,128)S(1)}, u32[]{:S(2)}, u32[]{:S(2)}) collective-permute-start(f32[3,64,128]{2,1,0:T(8,128)S(1)} %get-tuple-element.15), channel_id=1, source_target_pairs={{0,16},{16,32},{32,48},{48,64},{64,80},{80,96},{96,112},{112,128},... | collective-permute-start | bytes 294920 | tf_op jit(solution)/shard_map/ppermute | solution.py:231
  5.8 8.0 %collective-permute-start.1 = (f32[3,64,128]{2,1,0:T(8,128)S(1)}, f32[3,64,128]{2,1,0:T(8,128)S(1)}, u32[]{:S(2)}, u32[]{:S(2)}) collective-permute-start(f32[3,64,128]{2,1,0:T(8,128)S(1)} %get-tuple-element.16), channel_id=1, source_target_pairs={{16,0},{32,16},{48,32},{64,48},{80,64},{96,80},{112,96},{128,112},... | collective-permute-start | bytes 294920 | tf_op jit(solution)/shard_map/ppermute | solution.py:231
  13.9 6.3 %copy-start.1 = (bf16[256,256]{1,0:T(8,128)(2,1)S(1)}, bf16[256,256]{1,0:T(8,128)(2,1)}, u32[]{:S(2)}) copy-start(bf16[256,256]{1,0:T(8,128)(2,1)} %w2_ref.1) | copy-start | bytes 393220
  14.1 5.8 %copy-start.7 = (f32[54]{0:T(128)S(1)}, f32[54]{0:T(128)}, u32[]{:S(2)}) copy-start(f32[54]{0:T(128)} %param.21) | copy-start | bytes 652
  14.1 5.9 %copy-start.10 = (bf16[256,55]{0,1:T(8,128)(2,1)S(1)}, bf16[256,55]{0,1:T(8,128)(2,1)}, u32[]{:S(2)}) copy-start(bf16[256,55]{0,1:T(8,128)(2,1)} %param.16) | copy-start | bytes 84484
  14.2 7.3 %collective-permute-start.3 = (f32[64,128]{1,0:T(8,128)S(1)}, f32[64,128]{1,0:T(8,128)S(1)}, u32[]{:S(2)}, u32[]{:S(2)}) collective-permute-start(f32[64,128]{1,0:T(8,128)S(1)} %strip.1.own_ref), channel_id=1, source_target_pairs={{1,0},{2,1},{3,2},{4,3},{5,4},{6,5},{7,6},{8,7},{9,8},{10,9},{11,1... | collective-permute-start | bytes 98312 | tf_op jit(solution)/shard_map/ppermute | solution.py:231
  18.0 5.9 %collective-permute-start.2 = (f32[64,128]{1,0:T(8,128)S(1)}, f32[64,128]{1,0:T(8,128)S(1)}, u32[]{:S(2)}, u32[]{:S(2)}) collective-permute-start(f32[64,128]{1,0:T(8,128)S(1)} %strip.1.own_ref), channel_id=1, source_target_pairs={{0,1},{1,2},{2,3},{3,4},{4,5},{5,6},{6,7},{7,8},{8,9},{9,10},{10,1... | collective-permute-start | bytes 98312 | tf_op jit(solution)/shard_map/ppermute | solution.py:231
  20.1 0.7 %copy-start.2 = (bf16[54,256]{1,0:T(8,128)(2,1)S(1)}, bf16[54,256]{1,0:T(8,128)(2,1)}, u32[]{:S(2)}) copy-start(bf16[54,256]{1,0:T(8,128)(2,1)} %w3_ref.1) | copy-start | bytes 82948
  20.1 0.7 %copy-start.5 = (s32[8,128]{1,0:T(8,128)S(1)}, s32[8,128]{1,0:T(8,128)}, u32[]{:S(2)}) copy-start(s32[8,128]{1,0:T(8,128)} %act_ref.1) | copy-start | bytes 12292
  23.9 0.7 %copy-start.9 = (f32[256]{0:T(256)S(1)}, f32[256]{0:T(256)}, u32[]{:S(2)}) copy-start(f32[256]{0:T(256)} %param.19) | copy-start | bytes 3076
  23.9 0.7 %copy-start.6 = (f32[8,128]{1,0:T(8,128)S(1)}, f32[8,128]{1,0:T(8,128)}, u32[]{:S(2)}) copy-start(f32[8,128]{1,0:T(8,128)} %heat_ref.1) | copy-start | bytes 12292
  23.9 0.7 %copy-start.8 = (f32[256]{0:T(256)S(1)}, f32[256]{0:T(256)}, u32[]{:S(2)}) copy-start(f32[256]{0:T(256)} %param.17) | copy-start | bytes 3076

commit v2 on v1

v2 whole, which is shorter than its diff:
```python
import jax
import jax.numpy as jnp
from jax import lax
from jax.experimental import pallas as pl
from jax.experimental.pallas import tpu as pltpu
from jax.sharding import PartitionSpec as P

SUBSTEPS = 8
STEPS = 3
KINDS = 54
HID = 256
ROWS = 8
LANES = 128
CAP = 384
CHUNK = 128
CHANNELS = 64
DIFF, SPEED_C, SPEED_R, INSIDE = 54, 55, 56, 57
WIDE = 9
COST_PREPARE = 20_000_000
COST_MOVE = 20_000_000
chem_step = 0.0625
f32 = jnp.float32
bf16 = jnp.bfloat16


def iota(shape, axis):
    return lax.broadcasted_iota(jnp.int32, shape, axis)


def planes_kernel(y_hbm, d_hbm, v_hbm, all_ref, near_ref, far_ref, y_ref, d_ref, v_ref, sems):
    copies = [
        pltpu.make_async_copy(source, target, sems.at[k])
        for k, (source, target) in enumerate(((y_hbm, y_ref), (d_hbm, d_ref), (v_hbm, v_ref)))
    ]
    for copy in copies:
        copy.start()
    for r in range(ROWS):
        all_ref[r, INSIDE:CHANNELS, :] = jnp.ones((CHANNELS - INSIDE, LANES), f32)
    for copy in copies:
        copy.wait()
    for r in range(ROWS):
        all_ref[r, 0:KINDS, :] = y_ref[pl.ds(r, KINDS, stride=ROWS), :]
        all_ref[r, DIFF : DIFF + 1, :] = d_ref[r : r + 1, :]
        all_ref[r, SPEED_C : SPEED_C + 1, :] = v_ref[0, r : r + 1, :]
        all_ref[r, SPEED_R : SPEED_R + 1, :] = v_ref[1, r : r + 1, :]
    odd = lax.axis_index("row") % 2 == 1
    for k in range(STEPS):
        top, bottom = all_ref[k], all_ref[ROWS - STEPS + k]
        near_ref[k] = jnp.where(odd, top, bottom)
        far_ref[k] = jnp.where(odd, bottom, top)


def strip_kernel(all_ref, near_ref, far_ref, done_ref, low_ref, high_ref, left_ref, right_ref):
    odd = lax.axis_index("row") % 2 == 1
    for k in range(STEPS):
        near, far = near_ref[k], far_ref[k]
        low_ref[k] = jnp.where(odd, near, far)
        high_ref[k] = jnp.where(odd, far, near)
    lane = iota((CHANNELS, LANES), 1)
    left = jnp.broadcast_to(done_ref[0:1, :], (CHANNELS, LANES))
    right = jnp.zeros((CHANNELS, LANES), f32)
    for i in range(ROWS + 6):
        plane = low_ref[i] if i < STEPS else all_ref[i - STEPS] if i < STEPS + ROWS else high_ref[i - STEPS - ROWS]
        at = WIDE * i
        left = jnp.where((lane >= at) & (lane < at + WIDE), pltpu.roll(plane, (at + 3) % LANES, 1), left)
        at = (at - 3) % LANES
        hit = (lane - at) % LANES < WIDE
        right = jnp.where(hit, pltpu.roll(plane, (at + 6) % LANES, 1), right)
    left_ref[...] = left
    right_ref[...] = right


def prepare_kernel(
    act_ref, w1_ref, w2_ref, w3_ref, b1_in, b2_in, b3_in, heat_in,
    pick_ref, w1t_ref, w2t_ref, mix_ref, w3t_ref, bias_ref, b1_ref, b2_ref, b3_ref, heat_ref, done_ref,
):
    b1_ref[...] = b1_in[...]
    b2_ref[...] = b2_in[...]
    b3_ref[...] = b3_in[...]
    heat_ref[...] = heat_in[...]
    done_ref[...] = jnp.zeros(done_ref.shape, f32)
    act = act_ref[...].astype(f32)
    before = (iota((LANES, LANES), 0) < iota((LANES, LANES), 1)).astype(f32).astype(bf16)
    inner = jnp.dot(act.astype(bf16), before, preferred_element_type=f32)
    counts = jnp.broadcast_to(jnp.sum(act, axis=1, keepdims=True), (ROWS, LANES))
    row = iota((ROWS, LANES), 0)
    outer = jnp.zeros((ROWS, LANES), f32)
    for k in range(ROWS - 1):
        outer = outer + jnp.where(row > k, jnp.broadcast_to(counts[k : k + 1, :], (ROWS, LANES)), 0.0)
    slot = jnp.where(act > 0.0, inner + outer, -1.0).astype(jnp.int32)
    slots = iota((CAP, LANES), 0)
    for r in range(ROWS):
        hit = slots == jnp.broadcast_to(slot[r : r + 1, :], (CAP, LANES))
        pick_ref[:, r * LANES : (r + 1) * LANES] = jnp.where(hit, 1.0, 0.0).astype(bf16)
    w1t = w1_ref[...].astype(f32)
    w1t_ref[...] = jnp.zeros((2 * CHANNELS, HID), bf16)
    for k in range(2):
        w1t_ref[k * CHANNELS : k * CHANNELS + KINDS + 1, :] = w1t.astype(bf16)
    w2t_ref[...] = w2_ref[...].astype(f32).T.astype(bf16)
    w3t = w3_ref[...].astype(f32).T
    w3t_ref[...] = w3t.astype(bf16)
    part = w1t[0:KINDS, :]
    mix = jnp.dot(w3t.astype(bf16), part.astype(bf16), preferred_element_type=f32)
    mix_ref[...] = (chem_step * mix).astype(bf16)
    shifts = jnp.broadcast_to(b3_in[...], (KINDS, KINDS))
    same = iota((KINDS, KINDS), 0) == iota((KINDS, KINDS), 1)
    shifts = jnp.sum(jnp.where(same, shifts, 0.0), axis=1, keepdims=True)
    bias_ref[...] = chem_step * jnp.sum(part * shifts, axis=0, keepdims=True)


def face(d_low, d_high, u_low, u_high):
    d = 0.5 * (d_low + d_high)
    u = 0.5 * (u_low + u_high)
    return d - jnp.minimum(u, 0.0), d + jnp.maximum(u, 0.0)


def move_kernel(all_ref, low_ref, high_ref, moved_ref, base_ref, coef_ref, one_ref, two_ref):
    ahead, behind = LANES - 1, 1
    for k in range(4):
        base_ref[k, 0:8, :] = jnp.zeros((8, LANES), f32)
        base_ref[k, 22:32, :] = jnp.zeros((10, LANES), f32)
        for i in range(STEPS):
            base_ref[k, 8 + i : 9 + i, :] = low_ref[i, DIFF + k : DIFF + k + 1, :]
            base_ref[k, 19 + i : 20 + i, :] = high_ref[i, DIFF + k : DIFF + k + 1, :]
        for r in range(ROWS):
            base_ref[k, 11 + r : 12 + r, :] = all_ref[r, DIFF + k : DIFF + k + 1, :]
    d, u, v, inside = (base_ref[k, 8:24, :] for k in range(4))
    a_r, b_r = face(d, pltpu.roll(d, ahead, 1), u, pltpu.roll(u, ahead, 1))
    a_l, b_l = pltpu.roll(a_r, behind, 1), pltpu.roll(b_r, behind, 1)
    a_u, b_u = face(d, base_ref[0, 9:25, :], v, base_ref[2, 9:25, :])
    a_d, b_d = face(base_ref[0, 7:23, :], d, base_ref[2, 7:23, :], v)
    for k, c in enumerate((1.0 - b_r - a_l - b_u - a_d, a_r, b_l, a_u, b_d)):
        coef_ref[k] = inside * c

    def load(step, i):
        if step == 0:
            if i < STEPS:
                return low_ref[i, 0:56, :]
            if i < STEPS + ROWS:
                return all_ref[i - STEPS, 0:56, :]
            return high_ref[i - STEPS - ROWS, 0:56, :]
        return (one_ref if step % 2 else two_ref)[i]

    for step in range(STEPS):
        target = two_ref if step % 2 else one_ref
        for i in range(1 + step, 13 - step):
            mine = load(step, i)
            c = [jnp.broadcast_to(coef_ref[k, i : i + 1, :], (56, LANES)) for k in range(5)]
            new = (
                c[0] * mine
                + c[1] * pltpu.roll(mine, ahead, 1)
                + c[2] * pltpu.roll(mine, behind, 1)
                + c[3] * load(step, i + 1)
                + c[4] * load(step, i - 1)
            )
            if step < STEPS - 1:
                target[i] = new
            else:
                moved_ref[i - STEPS] = new


def move_strip(strip):
    ahead, behind = LANES - 1, 1
    d, u, v, inside = (strip[k : k + 1, :] for k in (DIFF, SPEED_C, SPEED_R, INSIDE))
    a_r, b_r = face(d, pltpu.roll(d, ahead, 1), u, pltpu.roll(u, ahead, 1))
    a_l, b_l = pltpu.roll(a_r, behind, 1), pltpu.roll(b_r, behind, 1)
    a_u, b_u = face(d, pltpu.roll(d, LANES - WIDE, 1), v, pltpu.roll(v, LANES - WIDE, 1))
    a_d, b_d = pltpu.roll(a_u, WIDE, 1), pltpu.roll(b_u, WIDE, 1)
    c = [jnp.broadcast_to(inside * x, (56, LANES)) for x in (1.0 - b_r - a_l - b_u - a_d, a_r, b_l, a_u, b_d)]
    strip = strip[0:56, :]
    for _ in range(STEPS):
        strip = (
            c[0] * strip
            + c[1] * pltpu.roll(strip, ahead, 1)
            + c[2] * pltpu.roll(strip, behind, 1)
            + c[3] * pltpu.roll(strip, LANES - WIDE, 1)
            + c[4] * pltpu.roll(strip, WIDE, 1)
        )
    return strip


def main_kernel(
    moved_ref, left_own, right_own, left_ref, right_ref,
    pick_ref, w1t_ref, w2t_ref, mix_ref, w3t_ref, bias_ref, b1_ref, b2_ref, b3_ref, heat_ref,
    out_ref, full_ref, feat_ref, pre_ref, sum_ref,
):
    lane = iota((CHANNELS, LANES), 1)
    left = move_strip(jnp.where(lane % WIDE < 3, left_ref[...], left_own[...]))
    right = move_strip(jnp.where((lane + 3) % LANES % WIDE < 6, right_own[...], right_ref[...]))
    lane = iota((56, LANES), 1)
    place = lane % WIDE
    edges = jnp.where((place >= 3) & (place < 6), left, right)
    outer = (lane < STEPS) | (lane >= LANES - STEPS)
    for r in range(ROWS):
        full_ref[r] = jnp.where(outer, pltpu.roll(edges, (2 * LANES - WIDE * (r + STEPS) - 3) % LANES, 1), moved_ref[r])

    sub = iota((56, LANES), 0)
    for r in range(ROWS):
        block = jnp.where(sub < KINDS, full_ref[r], 0.0)
        block = jnp.where(sub == KINDS, jnp.broadcast_to(heat_ref[r : r + 1, :], (56, LANES)), block)
        block = jnp.concatenate([block, jnp.zeros((8, LANES), f32)], 0)
        coarse = block.astype(bf16)
        fine = jnp.where(iota((CHANNELS, LANES), 0) < KINDS, block - coarse.astype(f32), 0.0).astype(bf16)
        feat_ref[0:CHANNELS, r * LANES : (r + 1) * LANES] = coarse
        feat_ref[CHANNELS:, r * LANES : (r + 1) * LANES] = fine
    slots = lax.dot_general(pick_ref[...], feat_ref[...], (((1,), (1,)), ((), ())), preferred_element_type=f32)
    for k in range(CAP // CHUNK):
        s = slice(k * CHUNK, (k + 1) * CHUNK)
        pre_ref[s, :] = jnp.dot(slots[s, :].astype(bf16), w1t_ref[...], preferred_element_type=f32) + b1_ref[...]
    for index in range(SUBSTEPS):
        for k in range(CAP // CHUNK):
            s = slice(k * CHUNK, (k + 1) * CHUNK)
            first = jnp.tanh(pre_ref[s, :]).astype(bf16)
            second = jnp.dot(first, w2t_ref[...], preferred_element_type=f32) + b2_ref[...]
            second = jnp.tanh(second).astype(bf16)
            wide = second.astype(f32)
            sum_ref[s, :] = wide if index == 0 else sum_ref[s, :] + wide
            if index < SUBSTEPS - 1:
                pre_ref[s, :] += jnp.dot(second, mix_ref[...], preferred_element_type=f32) + bias_ref[...]
    total = sum_ref[...]
    high = total.astype(bf16)
    low = (total - high.astype(f32)).astype(bf16)
    rate = jnp.dot(high, w3t_ref[...], preferred_element_type=f32) + jnp.dot(low, w3t_ref[...], preferred_element_type=f32)
    rate = chem_step * (rate + SUBSTEPS * b3_ref[...])
    rate = jnp.concatenate([rate, jnp.zeros((CAP, LANES - KINDS), f32)], 1).T[0:56, :]
    high = rate.astype(bf16)
    low = (rate - high.astype(f32)).astype(bf16)
    for r in range(ROWS):
        block = pick_ref[:, r * LANES : (r + 1) * LANES]
        gain = jnp.dot(high, block, preferred_element_type=f32) + jnp.dot(low, block, preferred_element_type=f32)
        out_ref[pl.ds(r, KINDS, stride=ROWS), :] = (full_ref[r] + gain)[0:KINDS, :]


def stay(x):
    return pltpu.with_memory_space_constraint(x, pltpu.HBM)


def call(kernel, shapes, operands, name, scratch=(), copies=0, cost=None):
    return pl.pallas_call(
        kernel,
        out_shape=[jax.ShapeDtypeStruct(s, t) for s, t in shapes],
        in_specs=[pl.BlockSpec(memory_space=pltpu.HBM if copies else pltpu.VMEM)] * len(operands),
        out_specs=[pl.BlockSpec(memory_space=pltpu.VMEM)] * len(shapes),
        scratch_shapes=[pltpu.VMEM(s, t) for s, t in scratch] + [pltpu.SemaphoreType.DMA((copies,))] * (copies > 0),
        compiler_params=pltpu.CompilerParams(vmem_limit_bytes=16 << 20),
        cost_estimate=cost and pl.CostEstimate(flops=cost, bytes_accessed=0, transcendentals=0),
        name=name,
    )(*operands)


def shards(y, d, v, heat, active, w1, b1, w2, b2, w3, b3):
    plane = (CHANNELS, LANES)
    edge = ((STEPS,) + plane, f32)
    tile = (ROWS, LANES)
    every, near, far = call(
        planes_kernel, [((ROWS,) + plane, f32), edge, edge], [stay(x) for x in (y.reshape(KINDS * ROWS, LANES), d, v)], "planes",
        scratch=[((KINDS * ROWS, LANES), f32), (tile, f32), ((2,) + tile, f32)], copies=3,
    )
    devices = lax.axis_size("row")
    far = lax.ppermute(far, "row", [(i, i + 1 if i % 2 else i - 1) for i in range(1, devices - 1)])
    near = lax.ppermute(near, "row", [(i, i ^ 1) for i in range(devices)])
    *picks, done = call(
        prepare_kernel,
        [
            ((CAP, ROWS * LANES), bf16), ((2 * CHANNELS, HID), bf16), ((HID, HID), bf16), ((HID, HID), bf16),
            ((HID, KINDS), bf16), ((1, HID), f32), ((1, HID), f32), ((1, HID), f32), ((1, KINDS), f32), (tile, f32),
            (tile, f32),
        ],
        (active, w1.T, w2, w3, b1[None], b2[None], b3[None], heat),
        "prepare",
        cost=COST_PREPARE,
    )
    low, high, left_own, right_own = call(
        strip_kernel, [edge, edge, (plane, f32), (plane, f32)], (every, near, far, done), "strip"
    )
    devices = lax.axis_size("col")
    up = [(i, i + 1) for i in range(devices - 1)]
    left = lax.ppermute(left_own, "col", up)
    right = lax.ppermute(right_own, "col", [(b, a) for a, b in up])
    (moved,) = call(
        move_kernel, [((ROWS, 56, LANES), f32)], (every, low, high), "move",
        scratch=[((4, 32, LANES), f32), ((5, 16, LANES), f32), ((14, 56, LANES), f32), ((14, 56, LANES), f32)],
        cost=COST_MOVE,
    )
    (out,) = call(
        main_kernel,
        [((KINDS * ROWS, LANES), f32)],
        (moved, left_own, right_own, left, right, *picks),
        "main",
        scratch=[
            ((ROWS, 56, LANES), f32), ((2 * CHANNELS, ROWS * LANES), bf16), ((CAP, HID), f32), ((CAP, HID), f32),
        ],
    )
    return out.reshape(KINDS, ROWS, LANES)


def solution(mesh):
    tile, rest = P("row", "col"), P()
    stack = P(None, "row", "col")
    in_specs = (stack, tile, stack, tile, tile, rest, rest, rest, rest, rest, rest)
    return jax.shard_map(shards, mesh=mesh, in_specs=in_specs, out_specs=stack, check_vma=False)
```

time: 30 us -> 28.3 us (0.943)
  the two profiles are of different devices: /device:TPU:409 before, /device:TPU:228 now
where the time goes in v2:
time: 28.3 us; the launch traced here: 28 us
  starting transfers between devices  13.9 us (49%)
  Pallas kernels  7.06 us (25%)
  waiting for transfers between devices  6.26 us (22%)
  local copies, waits for them, and re-layouts  0.64 us (2%)
    pallas_call x5, Pallas kernels, call(): pl.pallas_call(kernel, out_shape=[jax.ShapeDtypeStruct(s, t) for s, t in...  7.06 us
    ppermute x1, starting transfers between devices, shards(): left = lax.ppermute(left_own, 'col', up)  5.04 us
    ppermute x1, starting transfers between devices, shards(): lax.ppermute(far, 'row', [(i, i + 1 if i % 2 else i - 1) for i in range(1...  5 us
    ppermute x1, waiting for transfers between devices, shards(): right = lax.ppermute(right_own, 'col', [(b, a) for a, b in up])  4.5 us
    ppermute x1, starting transfers between devices, shards(): right = lax.ppermute(right_own, 'col', [(b, a) for a, b in up])  1.92 us
    ppermute x1, starting transfers between devices, shards(): near = lax.ppermute(near, 'row', [(i, i ^ 1) for i in range(devices)])  1.92 us
    ppermute x1, waiting for transfers between devices, shards(): lax.ppermute(far, 'row', [(i, i + 1 if i % 2 else i - 1) for i in range(1...  1.75 us
    unnamed x16, local copies, waits for them, and re-layouts  0.64 us
  transfers between devices with their start and end apart: 4, of which 2 were waited for; matrix products, arithmetic and copies ran while one was open for 0% of the time, Pallas kernels for 4%

profile of v2, /device:TPU:228, one launch (start us, length us, event | category | flops | bytes accessed | tf_op | source)
XLA Modules:
  0.0 28.0 jit_solution(13135686207429008745)
XLA Ops:
  0.0 0.0 copy-start
  0.0 0.0 copy-start.1
  0.0 0.0 copy-start.2
  0.0 0.0 copy-start.6
  0.0 0.0 copy-start.7
  0.0 1.1 %planes.1 = (f32[8,64,128]{2,1,0:T(8,128)S(1)}, f32[3,64,128]{2,1,0:T(8,128)S(1)}, f32[3,64,128]{2,1,0:T(8,128)S(1)}) custom-call(f32[432,128]{1,0:T(8,128)} %bitcast.10, f32[8,128]{1,0:T(8,128)} %d_hbm.1, f32[2,8,128]{2,1,0:T(8,128)} %v_hbm.1), custom_call_target="tpu_custom_call" | custom-call | tf_op jit(solution)/shard_map/planes/pallas_call | solution.py:239
  1.1 1.9 %collective-permute-start = (f32[3,64,128]{2,1,0:T(8,128)S(1)}, f32[3,64,128]{2,1,0:T(8,128)S(1)}, u32[]{:S(2)}, u32[]{:S(2)}) collective-permute-start(f32[3,64,128]{2,1,0:T(8,128)S(1)} %get-tuple-element.24), channel_id=1, source_target_pairs={{0,16},{16,0},{32,48},{48,32},{64,80},{80,64},{96,112},{112,96},{1... | collective-permute-start | bytes 294920 | tf_op jit(solution)/shard_map/ppermute | solution.py:261
  3.0 0.0 copy-start.4
  3.1 0.0 copy-start.3
  3.1 5.0 %collective-permute-start.1 = (f32[3,64,128]{2,1,0:T(8,128)S(1)}, f32[3,64,128]{2,1,0:T(8,128)S(1)}, u32[]{:S(2)}, u32[]{:S(2)}) collective-permute-start(f32[3,64,128]{2,1,0:T(8,128)S(1)} %get-tuple-element.25), channel_id=1, source_target_pairs={{16,32},{32,16},{48,64},{64,48},{80,96},{96,80},{112,128},{128,112... | collective-permute-start | bytes 294920 | tf_op jit(solution)/shard_map/ppermute | solution.py:260
  8.1 0.0 copy-start.5
  8.1 0.0 copy-done
  8.1 0.0 copy-done.1
  8.1 0.0 copy-done.2
  8.1 0.0 copy-done.6
  8.1 0.0 copy-done.7
  8.1 0.0 copy-done.4
  8.1 0.0 copy-done.3
  8.2 0.6 %copy-done.5 = f32[256]{0:T(256)S(1)} copy-done((f32[256]{0:T(256)S(1)}, f32[256]{0:T(256)}, u32[]{:S(2)}) %copy-start.5) | copy-done | bytes 1048
  8.8 0.6 %prepare.1 = (bf16[384,1024]{1,0:T(8,128)(2,1)S(1)}, bf16[128,256]{1,0:T(8,128)(2,1)S(1)}, bf16[256,256]{1,0:T(8,128)(2,1)S(1)}, bf16[256,256]{1,0:T(8,128)(2,1)...) custom-call(s32[8,128]{1,0:T(8,128)S(1)} %copy-done.3, ...), custom_call_target="tpu_custom_call" | custom-call | flops 20000000 | tf_op jit(solution)/shard_map/prepare/pallas_call | solution.py:239
  9.3 0.0 collective-permute-done.near_ref
  9.4 1.8 %collective-permute-done.1.far_ref = f32[3,64,128]{2,1,0:T(8,128)S(1)} collective-permute-done((f32[3,64,128]{2,1,0:T(8,128)S(1)}, f32[3,64,128]{2,1,0:T(8,128)S(1)}, u32[]{:S(2)}, u32[]{:S(2)}) %collective-permute-start.1) | collective-permute-done | bytes 98336 | tf_op jit(solution)/shard_map/ppermute | solution.py:260
  11.1 0.2 strip.1
  11.3 5.0 %collective-permute-start.2 = (f32[64,128]{1,0:T(8,128)S(1)}, f32[64,128]{1,0:T(8,128)S(1)}, u32[]{:S(2)}, u32[]{:S(2)}) collective-permute-start(f32[64,128]{1,0:T(8,128)S(1)} %get-tuple-element.29.left_own), channel_id=1, source_target_pairs={{0,1},{1,2},{2,3},{3,4},{4,5},{5,6},{6,7},{7,8},{8,9},{9,10},{10,1... | collective-permute-start | bytes 98312 | tf_op jit(solution)/shard_map/ppermute | solution.py:278
  16.4 1.9 %collective-permute-start.3 = (f32[64,128]{1,0:T(8,128)S(1)}, f32[64,128]{1,0:T(8,128)S(1)}, u32[]{:S(2)}, u32[]{:S(2)}) collective-permute-start(f32[64,128]{1,0:T(8,128)S(1)} %get-tuple-element.30.right_own), channel_id=1, source_target_pairs={{1,0},{2,1},{3,2},{4,3},{5,4},{6,5},{7,6},{8,7},{9,8},{10,9},{11,1... | collective-permute-start | bytes 98312 | tf_op jit(solution)/shard_map/ppermute | solution.py:279
  18.3 0.6 %move.1.moved_ref = f32[8,56,128]{2,1,0:T(8,128)S(1)} custom-call(f32[8,64,128]{2,1,0:T(8,128)S(1)} %get-tuple-element.23.all_ref, f32[3,64,128]{2,1,0:T(8,128)S(1)} %get-tuple-element.27.low_ref, f32[3,64,128]{2,1,0:T(8,128)S(1)} %get-tuple-element.28.high_ref), custom_call_target="tpu_custom_call" | custom-call | flops 20000000 | tf_op jit(solution)/shard_map/move/pallas_call | solution.py:239
  18.9 0.0 collective-permute-done.2.left_ref
  18.9 4.5 %collective-permute-done.3.right_ref = f32[64,128]{1,0:T(8,128)S(1)} collective-permute-done((f32[64,128]{1,0:T(8,128)S(1)}, f32[64,128]{1,0:T(8,128)S(1)}, u32[]{:S(2)}, u32[]{:S(2)}) %collective-permute-start.3) | collective-permute-done | bytes 32800 | tf_op jit(solution)/shard_map/ppermute | solution.py:279
  23.4 4.6 %main.1 = f32[432,128]{1,0:T(8,128)} custom-call(f32[8,56,128]{2,1,0:T(8,128)S(1)} %move.1.moved_ref, f32[64,128]{1,0:T(8,128)S(1)} %get-tuple-element.29.left_own, f32[64,128]{1,0:T(8,128)S(1)} %get-tuple-element.30.right_own, f32[64,128]{1,0:T(8,128)S(1)} %collective-permute-done.2.left_ref, f32[64,128]{1,0:T(8,128)S(1)} %collective-permute-done.3.right_ref, ...), custom_call_target="tpu_custom_call" | custom-call | tf_op jit(solution)/shard_map/main/pallas_call | solution.py:239
Async XLA Ops:
  0.0 8.1 %copy-start = (bf16[256,256]{1,0:T(8,128)(2,1)S(1)}, bf16[256,256]{1,0:T(8,128)(2,1)}, u32[]{:S(2)}) copy-start(bf16[256,256]{1,0:T(8,128)(2,1)} %w2_ref.1) | copy-start | bytes 393220
  0.0 8.1 %copy-start.1 = (bf16[256,55]{0,1:T(8,128)(2,1)S(1)}, bf16[256,55]{0,1:T(8,128)(2,1)}, u32[]{:S(2)}) copy-start(bf16[256,55]{0,1:T(8,128)(2,1)} %param.16) | copy-start | bytes 84484
  0.0 8.1 %copy-start.2 = (bf16[54,256]{1,0:T(8,128)(2,1)S(1)}, bf16[54,256]{1,0:T(8,128)(2,1)}, u32[]{:S(2)}) copy-start(bf16[54,256]{1,0:T(8,128)(2,1)} %w3_ref.1) | copy-start | bytes 82948
  0.0 8.1 %copy-start.6 = (f32[256]{0:T(256)S(1)}, f32[256]{0:T(256)}, u32[]{:S(2)}) copy-start(f32[256]{0:T(256)} %param.19) | copy-start | bytes 3076
  0.0 8.1 %copy-start.7 = (f32[54]{0:T(128)S(1)}, f32[54]{0:T(128)}, u32[]{:S(2)}) copy-start(f32[54]{0:T(128)} %param.21) | copy-start | bytes 652
  1.1 8.2 %collective-permute-start = (f32[3,64,128]{2,1,0:T(8,128)S(1)}, f32[3,64,128]{2,1,0:T(8,128)S(1)}, u32[]{:S(2)}, u32[]{:S(2)}) collective-permute-start(f32[3,64,128]{2,1,0:T(8,128)S(1)} %get-tuple-element.24), channel_id=1, source_target_pairs={{0,16},{16,0},{32,48},{48,32},{64,80},{80,64},{96,112},{112,96},{1... | collective-permute-start | bytes 294920 | tf_op jit(solution)/shard_map/ppermute | solution.py:261
  3.0 5.1 %copy-start.4 = (f32[8,128]{1,0:T(8,128)S(1)}, f32[8,128]{1,0:T(8,128)}, u32[]{:S(2)}) copy-start(f32[8,128]{1,0:T(8,128)} %heat_in.1) | copy-start | bytes 12292
  3.1 5.1 %copy-start.3 = (s32[8,128]{1,0:T(8,128)S(1)}, s32[8,128]{1,0:T(8,128)}, u32[]{:S(2)}) copy-start(s32[8,128]{1,0:T(8,128)} %act_ref.1) | copy-start | bytes 12292
  3.1 8.0 %collective-permute-start.1 = (f32[3,64,128]{2,1,0:T(8,128)S(1)}, f32[3,64,128]{2,1,0:T(8,128)S(1)}, u32[]{:S(2)}, u32[]{:S(2)}) collective-permute-start(f32[3,64,128]{2,1,0:T(8,128)S(1)} %get-tuple-element.25), channel_id=1, source_target_pairs={{16,32},{32,16},{48,64},{64,48},{80,96},{96,80},{112,128},{128,112... | collective-permute-start | bytes 294920 | tf_op jit(solution)/shard_map/ppermute | solution.py:260
  8.1 0.7 %copy-start.5 = (f32[256]{0:T(256)S(1)}, f32[256]{0:T(256)}, u32[]{:S(2)}) copy-start(f32[256]{0:T(256)} %param.17) | copy-start | bytes 3076
  11.3 7.6 %collective-permute-start.2 = (f32[64,128]{1,0:T(8,128)S(1)}, f32[64,128]{1,0:T(8,128)S(1)}, u32[]{:S(2)}, u32[]{:S(2)}) collective-permute-start(f32[64,128]{1,0:T(8,128)S(1)} %get-tuple-element.29.left_own), channel_id=1, source_target_pairs={{0,1},{1,2},{2,3},{3,4},{4,5},{5,6},{6,7},{7,8},{8,9},{9,10},{10,1... | collective-permute-start | bytes 98312 | tf_op jit(solution)/shard_map/ppermute | solution.py:278
  16.4 7.0 %collective-permute-start.3 = (f32[64,128]{1,0:T(8,128)S(1)}, f32[64,128]{1,0:T(8,128)S(1)}, u32[]{:S(2)}, u32[]{:S(2)}) collective-permute-start(f32[64,128]{1,0:T(8,128)S(1)} %get-tuple-element.30.right_own), channel_id=1, source_target_pairs={{1,0},{2,1},{3,2},{4,3},{5,4},{6,5},{7,6},{8,7},{9,8},{10,9},{11,1... | collective-permute-start | bytes 98312 | tf_op jit(solution)/shard_map/ppermute | solution.py:279

commit v3 on v2

--- a/solution.py
+++ b/solution.py
@@ -4,6 +4,7 @@
 from jax.experimental import pallas as pl
 from jax.experimental.pallas import tpu as pltpu
 from jax.sharding import PartitionSpec as P
+
 
 SUBSTEPS = 8
 STEPS = 3
@@ -235,7 +236,7 @@
     return pltpu.with_memory_space_constraint(x, pltpu.HBM)
 
 
-def call(kernel, shapes, operands, name, scratch=(), copies=0, cost=None):
+def call(kernel, shapes, operands, scratch=(), copies=0, cost=None):
     return pl.pallas_call(
         kernel,
         out_shape=[jax.ShapeDtypeStruct(s, t) for s, t in shapes],
@@ -244,7 +245,6 @@
         scratch_shapes=[pltpu.VMEM(s, t) for s, t in scratch] + [pltpu.SemaphoreType.DMA((copies,))] * (copies > 0),
         compiler_params=pltpu.CompilerParams(vmem_limit_bytes=16 << 20),
         cost_estimate=cost and pl.CostEstimate(flops=cost, bytes_accessed=0, transcendentals=0),
-        name=name,
     )(*operands)
 
 
@@ -253,7 +253,7 @@
     edge = ((STEPS,) + plane, f32)
     tile = (ROWS, LANES)
     every, near, far = call(
-        planes_kernel, [((ROWS,) + plane, f32), edge, edge], [stay(x) for x in (y.reshape(KINDS * ROWS, LANES), d, v)], "planes",
+        planes_kernel, [((ROWS,) + plane, f32), edge, edge], [stay(x) for x in (y.reshape(KINDS * ROWS, LANES), d, v)],
         scratch=[((KINDS * ROWS, LANES), f32), (tile, f32), ((2,) + tile, f32)], copies=3,
     )
     devices = lax.axis_size("row")
@@ -267,18 +267,17 @@
             (tile, f32),
         ],
         (active, w1.T, w2, w3, b1[None], b2[None], b3[None], heat),
-        "prepare",
         cost=COST_PREPARE,
     )
     low, high, left_own, right_own = call(
-        strip_kernel, [edge, edge, (plane, f32), (plane, f32)], (every, near, far, done), "strip"
+        strip_kernel, [edge, edge, (plane, f32), (plane, f32)], (every, near, far, done)
     )
     devices = lax.axis_size("col")
     up = [(i, i + 1) for i in range(devices - 1)]
+    right = lax.ppermute(right_own, "col", [(b, a) for a, b in up])
     left = lax.ppermute(left_own, "col", up)
-    right = lax.ppermute(right_own, "col", [(b, a) for a, b in up])
     (moved,) = call(
-        move_kernel, [((ROWS, 56, LANES), f32)], (every, low, high), "move",
+        move_kernel, [((ROWS, 56, LANES), f32)], (every, low, high),
         scratch=[((4, 32, LANES), f32), ((5, 16, LANES), f32), ((14, 56, LANES), f32), ((14, 56, LANES), f32)],
         cost=COST_MOVE,
     )
@@ -286,7 +285,6 @@
         main_kernel,
         [((KINDS * ROWS, LANES), f32)],
         (moved, left_own, right_own, left, right, *picks),
-        "main",
         scratch=[
             ((ROWS, 56, LANES), f32), ((2 * CHANNELS, ROWS * LANES), bf16), ((CAP, HID), f32), ((CAP, HID), f32),
         ],

time: 28.3 us -> 28.3 us (level)
  no operation moved by 1% of the time
where the time goes in v3:
time: 28.3 us; the launch traced here: 28 us
  starting transfers between devices  13.9 us (49%)
  Pallas kernels  7.06 us (25%)
  waiting for transfers between devices  6.26 us (22%)
  local copies, waits for them, and re-layouts  0.64 us (2%)
    pallas_call x5, Pallas kernels, call(): pl.pallas_call(kernel, out_shape=[jax.ShapeDtypeStruct(s, t) for s, t in...  7.06 us
    ppermute x1, starting transfers between devices, shards(): left = lax.ppermute(left_own, 'col', up)  5.04 us
    ppermute x1, starting transfers between devices, shards(): lax.ppermute(far, 'row', [(i, i + 1 if i % 2 else i - 1) for i in range(1...  5 us
    ppermute x1, waiting for transfers between devices, shards(): right = lax.ppermute(right_own, 'col', [(b, a) for a, b in up])  4.5 us
    ppermute x1, starting transfers between devices, shards(): right = lax.ppermute(right_own, 'col', [(b, a) for a, b in up])  1.92 us
    ppermute x1, starting transfers between devices, shards(): near = lax.ppermute(near, 'row', [(i, i ^ 1) for i in range(devices)])  1.92 us
    ppermute x1, waiting for transfers between devices, shards(): lax.ppermute(far, 'row', [(i, i + 1 if i % 2 else i - 1) for i in range(1...  1.75 us
    unnamed x16, local copies, waits for them, and re-layouts  0.64 us
  transfers between devices with their start and end apart: 4, of which 2 were waited for; matrix products, arithmetic and copies ran while one was open for 0% of the time, Pallas kernels for 4%

profile of v3, /device:TPU:228, one launch (start us, length us, event | category | flops | bytes accessed | tf_op | source)
XLA Modules:
  0.0 28.0 jit_solution(13135686207429008745)
XLA Ops:
  0.0 0.0 copy-start
  0.0 0.0 copy-start.1
  0.0 0.0 copy-start.2
  0.0 0.0 copy-start.6
  0.0 0.0 copy-start.7
  0.0 1.1 %shard_map.109 = (f32[8,64,128]{2,1,0:T(8,128)S(1)}, f32[3,64,128]{2,1,0:T(8,128)S(1)}, f32[3,64,128]{2,1,0:T(8,128)S(1)}) custom-call(f32[432,128]{1,0:T(8,128)} %bitcast.10, f32[8,128]{1,0:T(8,128)} %d_hbm.1, f32[2,8,128]{2,1,0:T(8,128)} %v_hbm.1), custom_call_target="tpu_custom_call" | custom-call | tf_op jit(solution)/shard_map/pallas_call | solution.py:240
  1.1 1.9 %collective-permute-start = (f32[3,64,128]{2,1,0:T(8,128)S(1)}, f32[3,64,128]{2,1,0:T(8,128)S(1)}, u32[]{:S(2)}, u32[]{:S(2)}) collective-permute-start(f32[3,64,128]{2,1,0:T(8,128)S(1)} %get-tuple-element.24), channel_id=1, source_target_pairs={{0,16},{16,0},{32,48},{48,32},{64,80},{80,64},{96,112},{112,96},{1... | collective-permute-start | bytes 294920 | tf_op jit(solution)/shard_map/ppermute | solution.py:261
  3.0 0.0 copy-start.4
  3.1 0.0 copy-start.3
  3.1 5.0 %collective-permute-start.1 = (f32[3,64,128]{2,1,0:T(8,128)S(1)}, f32[3,64,128]{2,1,0:T(8,128)S(1)}, u32[]{:S(2)}, u32[]{:S(2)}) collective-permute-start(f32[3,64,128]{2,1,0:T(8,128)S(1)} %get-tuple-element.25), channel_id=1, source_target_pairs={{16,32},{32,16},{48,64},{64,48},{80,96},{96,80},{112,128},{128,112... | collective-permute-start | bytes 294920 | tf_op jit(solution)/shard_map/ppermute | solution.py:260
  8.1 0.0 copy-start.5
  8.1 0.0 copy-done
  8.1 0.0 copy-done.1
  8.1 0.0 copy-done.2
  8.1 0.0 copy-done.6
  8.1 0.0 copy-done.7
  8.1 0.0 copy-done.4
  8.1 0.0 copy-done.3
  8.2 0.6 %copy-done.5 = f32[256]{0:T(256)S(1)} copy-done((f32[256]{0:T(256)S(1)}, f32[256]{0:T(256)}, u32[]{:S(2)}) %copy-start.5) | copy-done | bytes 1048
  8.8 0.6 %shard_map.110 = (bf16[384,1024]{1,0:T(8,128)(2,1)S(1)}, bf16[128,256]{1,0:T(8,128)(2,1)S(1)}, bf16[256,256]{1,0:T(8,128)(2,1)S(1)}, bf16[256,256]{1,0:T(8,128)(...) custom-call(s32[8,128]{1,0:T(8,128)S(1)} %copy-done.3, ...), custom_call_target="tpu_custom_call" | custom-call | flops 20000000 | tf_op jit(solution)/shard_map/pallas_call | solution.py:240
  9.3 0.0 collective-permute-done.near_ref
  9.4 1.8 %collective-permute-done.1.far_ref = f32[3,64,128]{2,1,0:T(8,128)S(1)} collective-permute-done((f32[3,64,128]{2,1,0:T(8,128)S(1)}, f32[3,64,128]{2,1,0:T(8,128)S(1)}, u32[]{:S(2)}, u32[]{:S(2)}) %collective-permute-start.1) | collective-permute-done | bytes 98336 | tf_op jit(solution)/shard_map/ppermute | solution.py:260
  11.1 0.2 shard_map.111
  11.3 5.0 %collective-permute-start.2 = (f32[64,128]{1,0:T(8,128)S(1)}, f32[64,128]{1,0:T(8,128)S(1)}, u32[]{:S(2)}, u32[]{:S(2)}) collective-permute-start(f32[64,128]{1,0:T(8,128)S(1)} %get-tuple-element.29.left_own), channel_id=1, source_target_pairs={{0,1},{1,2},{2,3},{3,4},{4,5},{5,6},{6,7},{7,8},{8,9},{9,10},{10,1... | collective-permute-start | bytes 98312 | tf_op jit(solution)/shard_map/ppermute | solution.py:278
  16.4 1.9 %collective-permute-start.3 = (f32[64,128]{1,0:T(8,128)S(1)}, f32[64,128]{1,0:T(8,128)S(1)}, u32[]{:S(2)}, u32[]{:S(2)}) collective-permute-start(f32[64,128]{1,0:T(8,128)S(1)} %get-tuple-element.30.right_own), channel_id=1, source_target_pairs={{1,0},{2,1},{3,2},{4,3},{5,4},{6,5},{7,6},{8,7},{9,8},{10,9},{11,1... | collective-permute-start | bytes 98312 | tf_op jit(solution)/shard_map/ppermute | solution.py:277
  18.3 0.6 %shard_map.112.moved_ref = f32[8,56,128]{2,1,0:T(8,128)S(1)} custom-call(f32[8,64,128]{2,1,0:T(8,128)S(1)} %get-tuple-element.23.all_ref, f32[3,64,128]{2,1,0:T(8,128)S(1)} %get-tuple-element.27.low_ref, f32[3,64,128]{2,1,0:T(8,128)S(1)} %get-tuple-element.28.high_ref), custom_call_target="tpu_custom_call" | custom-call | flops 20000000 | tf_op jit(solution)/shard_map/pallas_call | solution.py:240
  18.9 0.0 collective-permute-done.2.left_ref
  18.9 4.5 %collective-permute-done.3.right_ref = f32[64,128]{1,0:T(8,128)S(1)} collective-permute-done((f32[64,128]{1,0:T(8,128)S(1)}, f32[64,128]{1,0:T(8,128)S(1)}, u32[]{:S(2)}, u32[]{:S(2)}) %collective-permute-start.3) | collective-permute-done | bytes 32800 | tf_op jit(solution)/shard_map/ppermute | solution.py:277
  23.4 4.6 %shard_map.113 = f32[432,128]{1,0:T(8,128)} custom-call(f32[8,56,128]{2,1,0:T(8,128)S(1)} %shard_map.112.moved_ref, f32[64,128]{1,0:T(8,128)S(1)} %get-tuple-element.29.left_own, f32[64,128]{1,0:T(8,128)S(1)} %get-tuple-element.30.right_own, f32[64,128]{1,0:T(8,128)S(1)} %collective-permute-done.2.left_ref, f32[64,128]{1,0:T(8,128)S(1)} %collective-permute-done.3.right_ref, ...), custom_call_target="tpu_custom_call" | custom-call | tf_op jit(solution)/shard_map/pallas_call | solution.py:240
Async XLA Ops:
  0.0 8.1 %copy-start = (bf16[256,256]{1,0:T(8,128)(2,1)S(1)}, bf16[256,256]{1,0:T(8,128)(2,1)}, u32[]{:S(2)}) copy-start(bf16[256,256]{1,0:T(8,128)(2,1)} %w2_ref.1) | copy-start | bytes 393220
  0.0 8.1 %copy-start.1 = (bf16[256,55]{0,1:T(8,128)(2,1)S(1)}, bf16[256,55]{0,1:T(8,128)(2,1)}, u32[]{:S(2)}) copy-start(bf16[256,55]{0,1:T(8,128)(2,1)} %param.16) | copy-start | bytes 84484
  0.0 8.1 %copy-start.2 = (bf16[54,256]{1,0:T(8,128)(2,1)S(1)}, bf16[54,256]{1,0:T(8,128)(2,1)}, u32[]{:S(2)}) copy-start(bf16[54,256]{1,0:T(8,128)(2,1)} %w3_ref.1) | copy-start | bytes 82948
  0.0 8.1 %copy-start.6 = (f32[256]{0:T(256)S(1)}, f32[256]{0:T(256)}, u32[]{:S(2)}) copy-start(f32[256]{0:T(256)} %param.19) | copy-start | bytes 3076
  0.0 8.1 %copy-start.7 = (f32[54]{0:T(128)S(1)}, f32[54]{0:T(128)}, u32[]{:S(2)}) copy-start(f32[54]{0:T(128)} %param.21) | copy-start | bytes 652
  1.1 8.2 %collective-permute-start = (f32[3,64,128]{2,1,0:T(8,128)S(1)}, f32[3,64,128]{2,1,0:T(8,128)S(1)}, u32[]{:S(2)}, u32[]{:S(2)}) collective-permute-start(f32[3,64,128]{2,1,0:T(8,128)S(1)} %get-tuple-element.24), channel_id=1, source_target_pairs={{0,16},{16,0},{32,48},{48,32},{64,80},{80,64},{96,112},{112,96},{1... | collective-permute-start | bytes 294920 | tf_op jit(solution)/shard_map/ppermute | solution.py:261
  3.0 5.1 %copy-start.4 = (f32[8,128]{1,0:T(8,128)S(1)}, f32[8,128]{1,0:T(8,128)}, u32[]{:S(2)}) copy-start(f32[8,128]{1,0:T(8,128)} %heat_in.1) | copy-start | bytes 12292
  3.1 5.1 %copy-start.3 = (s32[8,128]{1,0:T(8,128)S(1)}, s32[8,128]{1,0:T(8,128)}, u32[]{:S(2)}) copy-start(s32[8,128]{1,0:T(8,128)} %act_ref.1) | copy-start | bytes 12292
  3.1 8.0 %collective-permute-start.1 = (f32[3,64,128]{2,1,0:T(8,128)S(1)}, f32[3,64,128]{2,1,0:T(8,128)S(1)}, u32[]{:S(2)}, u32[]{:S(2)}) collective-permute-start(f32[3,64,128]{2,1,0:T(8,128)S(1)} %get-tuple-element.25), channel_id=1, source_target_pairs={{16,32},{32,16},{48,64},{64,48},{80,96},{96,80},{112,128},{128,112... | collective-permute-start | bytes 294920 | tf_op jit(solution)/shard_map/ppermute | solution.py:260
  8.1 0.7 %copy-start.5 = (f32[256]{0:T(256)S(1)}, f32[256]{0:T(256)}, u32[]{:S(2)}) copy-start(f32[256]{0:T(256)} %param.17) | copy-start | bytes 3076
  11.3 7.6 %collective-permute-start.2 = (f32[64,128]{1,0:T(8,128)S(1)}, f32[64,128]{1,0:T(8,128)S(1)}, u32[]{:S(2)}, u32[]{:S(2)}) collective-permute-start(f32[64,128]{1,0:T(8,128)S(1)} %get-tuple-element.29.left_own), channel_id=1, source_target_pairs={{0,1},{1,2},{2,3},{3,4},{4,5},{5,6},{6,7},{7,8},{8,9},{9,10},{10,1... | collective-permute-start | bytes 98312 | tf_op jit(solution)/shard_map/ppermute | solution.py:278
  16.4 7.0 %collective-permute-start.3 = (f32[64,128]{1,0:T(8,128)S(1)}, f32[64,128]{1,0:T(8,128)S(1)}, u32[]{:S(2)}, u32[]{:S(2)}) collective-permute-start(f32[64,128]{1,0:T(8,128)S(1)} %get-tuple-element.30.right_own), channel_id=1, source_target_pairs={{1,0},{2,1},{3,2},{4,3},{5,4},{6,5},{7,6},{8,7},{9,8},{10,9},{11,1... | collective-permute-start | bytes 98312 | tf_op jit(solution)/shard_map/ppermute | solution.py:277

commit v4 on v3

--- a/solution.py
+++ b/solution.py
@@ -13,7 +13,7 @@
 ROWS = 8
 LANES = 128
 CAP = 384
-CHUNK = 128
+CHUNK = 192
 CHANNELS = 64
 DIFF, SPEED_C, SPEED_R, INSIDE = 54, 55, 56, 57
 WIDE = 9
@@ -28,11 +28,15 @@
     return lax.broadcasted_iota(jnp.int32, shape, axis)
 
 
-def planes_kernel(y_hbm, d_hbm, v_hbm, all_ref, near_ref, far_ref, y_ref, d_ref, v_ref, sems):
-    copies = [
-        pltpu.make_async_copy(source, target, sems.at[k])
-        for k, (source, target) in enumerate(((y_hbm, y_ref), (d_hbm, d_ref), (v_hbm, v_ref)))
-    ]
+def planes_kernel(
+    y_hbm, d_hbm, v_hbm, act_hbm, heat_hbm, b1_hbm, b2_hbm, b3_hbm,
+    all_ref, near_ref, far_ref, act_ref, heat_ref, b1_ref, b2_ref, b3_ref, y_ref, d_ref, v_ref, sems,
+):
+    pairs = (
+        (y_hbm, y_ref), (d_hbm, d_ref), (v_hbm, v_ref), (act_hbm, act_ref), (heat_hbm, heat_ref),
+        (b1_hbm, b1_ref), (b2_hbm, b2_ref), (b3_hbm, b3_ref),
+    )
+    copies = [pltpu.make_async_copy(source, target, sems.at[k]) for k, (source, target) in enumerate(pairs)]
     for copy in copies:
         copy.start()
     for r in range(ROWS):
@@ -51,14 +55,14 @@
         far_ref[k] = jnp.where(odd, bottom, top)
 
 
-def strip_kernel(all_ref, near_ref, far_ref, done_ref, low_ref, high_ref, left_ref, right_ref):
+def strip_kernel(all_ref, near_ref, far_ref, token_ref, low_ref, high_ref, first_ref, second_ref):
     odd = lax.axis_index("row") % 2 == 1
     for k in range(STEPS):
         near, far = near_ref[k], far_ref[k]
         low_ref[k] = jnp.where(odd, near, far)
         high_ref[k] = jnp.where(odd, far, near)
     lane = iota((CHANNELS, LANES), 1)
-    left = jnp.broadcast_to(done_ref[0:1, :], (CHANNELS, LANES))
+    left = jnp.broadcast_to(token_ref[0:1, :], (CHANNELS, LANES))
     right = jnp.zeros((CHANNELS, LANES), f32)
     for i in range(ROWS + 6):
         plane = low_ref[i] if i < STEPS else all_ref[i - STEPS] if i < STEPS + ROWS else high_ref[i - STEPS - ROWS]
@@ -67,19 +71,15 @@
         at = (at - 3) % LANES
         hit = (lane - at) % LANES < WIDE
         right = jnp.where(hit, pltpu.roll(plane, (at + 6) % LANES, 1), right)
-    left_ref[...] = left
-    right_ref[...] = right
+    odd = lax.axis_index("col") % 2 == 1
+    first_ref[...] = jnp.where(odd, right, left)
+    second_ref[...] = jnp.where(odd, left, right)
 
 
 def prepare_kernel(
-    act_ref, w1_ref, w2_ref, w3_ref, b1_in, b2_in, b3_in, heat_in,
-    pick_ref, w1t_ref, w2t_ref, mix_ref, w3t_ref, bias_ref, b1_ref, b2_ref, b3_ref, heat_ref, done_ref,
+    act_ref, w1_ref, w2_ref, w3_ref, b3_ref, pick_ref, w1t_ref, w2t_ref, mix_ref, w3t_ref, bias_ref, token_ref
 ):
-    b1_ref[...] = b1_in[...]
-    b2_ref[...] = b2_in[...]
-    b3_ref[...] = b3_in[...]
-    heat_ref[...] = heat_in[...]
-    done_ref[...] = jnp.zeros(done_ref.shape, f32)
+    token_ref[...] = jnp.zeros(token_ref.shape, f32)
     act = act_ref[...].astype(f32)
     before = (iota((LANES, LANES), 0) < iota((LANES, LANES), 1)).astype(f32).astype(bf16)
     inner = jnp.dot(act.astype(bf16), before, preferred_element_type=f32)
@@ -103,7 +103,7 @@
     part = w1t[0:KINDS, :]
     mix = jnp.dot(w3t.astype(bf16), part.astype(bf16), preferred_element_type=f32)
     mix_ref[...] = (chem_step * mix).astype(bf16)
-    shifts = jnp.broadcast_to(b3_in[...], (KINDS, KINDS))
+    shifts = jnp.broadcast_to(b3_ref[...], (KINDS, KINDS))
     same = iota((KINDS, KINDS), 0) == iota((KINDS, KINDS), 1)
     shifts = jnp.sum(jnp.where(same, shifts, 0.0), axis=1, keepdims=True)
     bias_ref[...] = chem_step * jnp.sum(part * shifts, axis=0, keepdims=True)
@@ -181,13 +181,17 @@
 
 
 def main_kernel(
-    moved_ref, left_own, right_own, left_ref, right_ref,
+    moved_ref, first_ref, second_ref, early_ref, late_ref,
     pick_ref, w1t_ref, w2t_ref, mix_ref, w3t_ref, bias_ref, b1_ref, b2_ref, b3_ref, heat_ref,
     out_ref, full_ref, feat_ref, pre_ref, sum_ref,
 ):
     lane = iota((CHANNELS, LANES), 1)
-    left = move_strip(jnp.where(lane % WIDE < 3, left_ref[...], left_own[...]))
-    right = move_strip(jnp.where((lane + 3) % LANES % WIDE < 6, right_own[...], right_ref[...]))
+    odd = lax.axis_index("col") % 2 == 1
+    first, second, early, late = first_ref[...], second_ref[...], early_ref[...], late_ref[...]
+    left = jnp.where(lane % WIDE < 3, jnp.where(odd, early, late), jnp.where(odd, second, first))
+    inner = (lane + 3) % LANES % WIDE < 6
+    right = jnp.where(inner, jnp.where(odd, first, second), jnp.where(odd, late, early))
+    left, right = move_strip(left), move_strip(right)
     lane = iota((56, LANES), 1)
     place = lane % WIDE
     edges = jnp.where((place >= 3) & (place < 6), left, right)
@@ -208,28 +212,31 @@
     for k in range(CAP // CHUNK):
         s = slice(k * CHUNK, (k + 1) * CHUNK)
         pre_ref[s, :] = jnp.dot(slots[s, :].astype(bf16), w1t_ref[...], preferred_element_type=f32) + b1_ref[...]
+    parts = [slice(k * CHUNK, (k + 1) * CHUNK) for k in range(CAP // CHUNK)]
     for index in range(SUBSTEPS):
-        for k in range(CAP // CHUNK):
-            s = slice(k * CHUNK, (k + 1) * CHUNK)
-            first = jnp.tanh(pre_ref[s, :]).astype(bf16)
-            second = jnp.dot(first, w2t_ref[...], preferred_element_type=f32) + b2_ref[...]
-            second = jnp.tanh(second).astype(bf16)
-            wide = second.astype(f32)
+        first = [jnp.tanh(pre_ref[s, :]).astype(bf16) for s in parts]
+        second = [jnp.dot(h, w2t_ref[...], preferred_element_type=f32) + b2_ref[...] for h in first]
+        second = [jnp.tanh(h).astype(bf16) for h in second]
+        for s, h in zip(parts, second):
+            wide = h.astype(f32)
             sum_ref[s, :] = wide if index == 0 else sum_ref[s, :] + wide
             if index < SUBSTEPS - 1:
-                pre_ref[s, :] += jnp.dot(second, mix_ref[...], preferred_element_type=f32) + bias_ref[...]
+                pre_ref[s, :] += jnp.dot(h, mix_ref[...], preferred_element_type=f32) + bias_ref[...]
     total = sum_ref[...]
     high = total.astype(bf16)
     low = (total - high.astype(f32)).astype(bf16)
     rate = jnp.dot(high, w3t_ref[...], preferred_element_type=f32) + jnp.dot(low, w3t_ref[...], preferred_element_type=f32)
     rate = chem_step * (rate + SUBSTEPS * b3_ref[...])
-    rate = jnp.concatenate([rate, jnp.zeros((CAP, LANES - KINDS), f32)], 1).T[0:56, :]
+    rate = jnp.concatenate([rate, jnp.zeros((CAP, LANES - KINDS), f32)], 1).T[0:CHANNELS, :]
     high = rate.astype(bf16)
     low = (rate - high.astype(f32)).astype(bf16)
-    for r in range(ROWS):
-        block = pick_ref[:, r * LANES : (r + 1) * LANES]
-        gain = jnp.dot(high, block, preferred_element_type=f32) + jnp.dot(low, block, preferred_element_type=f32)
-        out_ref[pl.ds(r, KINDS, stride=ROWS), :] = (full_ref[r] + gain)[0:KINDS, :]
+    both = jnp.concatenate([high, low], 0)
+    for r in range(0, ROWS, 2):
+        gain = jnp.dot(both, pick_ref[:, r * LANES : (r + 2) * LANES], preferred_element_type=f32)
+        gain = gain[0:CHANNELS] + gain[CHANNELS:]
+        for k in range(2):
+            block = full_ref[r + k] + gain[0:56, k * LANES : (k + 1) * LANES]
+            out_ref[pl.ds(r + k, KINDS, stride=ROWS), :] = block[0:KINDS]
 
 
 def stay(x):
@@ -248,34 +255,40 @@
     )(*operands)
 
 
+def swaps(devices, first):
+    low = range(first, devices - 1, 2)
+    return [(i, i + 1) for i in low] + [(i + 1, i) for i in low]
+
+
 def shards(y, d, v, heat, active, w1, b1, w2, b2, w3, b3):
     plane = (CHANNELS, LANES)
     edge = ((STEPS,) + plane, f32)
     tile = (ROWS, LANES)
-    every, near, far = call(
-        planes_kernel, [((ROWS,) + plane, f32), edge, edge], [stay(x) for x in (y.reshape(KINDS * ROWS, LANES), d, v)],
-        scratch=[((KINDS * ROWS, LANES), f32), (tile, f32), ((2,) + tile, f32)], copies=3,
+    every, near, far, active, heat, b1, b2, b3 = call(
+        planes_kernel,
+        [
+            ((ROWS,) + plane, f32), edge, edge, (tile, jnp.int32), (tile, f32),
+            ((1, HID), f32), ((1, HID), f32), ((1, KINDS), f32),
+        ],
+        [stay(x) for x in (y.reshape(KINDS * ROWS, LANES), d, v, active, heat, b1[None], b2[None], b3[None])],
+        scratch=[((KINDS * ROWS, LANES), f32), (tile, f32), ((2,) + tile, f32)], copies=8,
     )
     devices = lax.axis_size("row")
-    far = lax.ppermute(far, "row", [(i, i + 1 if i % 2 else i - 1) for i in range(1, devices - 1)])
-    near = lax.ppermute(near, "row", [(i, i ^ 1) for i in range(devices)])
-    *picks, done = call(
+    far = lax.ppermute(far, "row", swaps(devices, 1))
+    near = lax.ppermute(near, "row", swaps(devices, 0))
+    *picks, token = call(
         prepare_kernel,
         [
             ((CAP, ROWS * LANES), bf16), ((2 * CHANNELS, HID), bf16), ((HID, HID), bf16), ((HID, HID), bf16),
-            ((HID, KINDS), bf16), ((1, HID), f32), ((1, HID), f32), ((1, HID), f32), ((1, KINDS), f32), (tile, f32),
-            (tile, f32),
+            ((HID, KINDS), bf16), ((1, HID), f32), (tile, f32),
         ],
-        (active, w1.T, w2, w3, b1[None], b2[None], b3[None], heat),
+        (active, w1.T, w2, w3, b3),
         cost=COST_PREPARE,
     )
-    low, high, left_own, right_own = call(
-        strip_kernel, [edge, edge, (plane, f32), (plane, f32)], (every, near, far, done)
-    )
+    low, high, first, second = call(strip_kernel, [edge, edge, (plane, f32), (plane, f32)], (every, near, far, token))
     devices = lax.axis_size("col")
-    up = [(i, i + 1) for i in range(devices - 1)]
-    right = lax.ppermute(right_own, "col", [(b, a) for a, b in up])
-    left = lax.ppermute(left_own, "col", up)
+    early = lax.ppermute(first, "col", swaps(devices, 0))
+    late = lax.ppermute(second, "col", swaps(devices, 1))
     (moved,) = call(
         move_kernel, [((ROWS, 56, LANES), f32)], (every, low, high),
         scratch=[((4, 32, LANES), f32), ((5, 16, LANES), f32), ((14, 56, LANES), f32), ((14, 56, LANES), f32)],
@@ -284,7 +297,7 @@
     (out,) = call(
         main_kernel,
         [((KINDS * ROWS, LANES), f32)],
-        (moved, left_own, right_own, left, right, *picks),
+        (moved, first, second, early, late, *picks, b1, b2, b3, heat),
         scratch=[
             ((ROWS, 56, LANES), f32), ((2 * CHANNELS, ROWS * LANES), bf16), ((CAP, HID), f32), ((CAP, HID), f32),
         ],

time: 28.3 us -> 26.5 us (0.936)
  the two profiles are of different devices: /device:TPU:228 before, /device:TPU:134 now
where the time goes in v4:
time: 26.5 us; the launch traced here: 26.3 us
  starting transfers between devices  13 us (49%)
  Pallas kernels  6.63 us (25%)
  waiting for transfers between devices  6.61 us (25%)
    pallas_call x5, Pallas kernels, call(): pl.pallas_call(kernel, out_shape=[jax.ShapeDtypeStruct(s, t) for s, t in...  6.63 us
    ppermute x1, starting transfers between devices, shards(): far = lax.ppermute(far, 'row', swaps(devices, 1))  5.29 us
    ppermute x1, waiting for transfers between devices, shards(): late = lax.ppermute(second, 'col', swaps(devices, 1))  4.5 us
    ppermute x1, starting transfers between devices, shards(): early = lax.ppermute(first, 'col', swaps(devices, 0))  3.83 us
    ppermute x1, waiting for transfers between devices, shards(): far = lax.ppermute(far, 'row', swaps(devices, 1))  2.11 us
    ppermute x1, starting transfers between devices, shards(): near = lax.ppermute(near, 'row', swaps(devices, 0))  1.92 us
    ppermute x1, starting transfers between devices, shards(): late = lax.ppermute(second, 'col', swaps(devices, 1))  1.92 us
  transfers between devices with their start and end apart: 4, of which 2 were waited for; matrix products, arithmetic and copies ran while one was open for 0% of the time, Pallas kernels for 4%

profile of v4, /device:TPU:134, one launch (start us, length us, event | category | flops | bytes accessed | tf_op | source)
XLA Modules:
  0.0 26.3 jit_solution(15687686365061022734)
XLA Ops:
  0.0 0.0 copy-start
  0.0 0.0 copy-start.1
  0.0 0.0 copy-start.2
  0.0 1.1 %shard_map.109 = (f32[8,64,128]{2,1,0:T(8,128)S(1)}, f32[3,64,128]{2,1,0:T(8,128)S(1)}, f32[3,64,128]{2,1,0:T(8,128)S(1)}, s32[8,128]{1,0:T(8,128)S(1)}, f32[8,1...) custom-call(f32[432,128]{1,0:T(8,128)} %bitcast.7, f32[8,128]{1,0:T(8,128)} %d_hbm.1, ...), custom_call_target="tpu_custom_call" | custom-call | tf_op jit(solution)/shard_map/pallas_call | solution.py:247
  1.1 1.9 %collective-permute-start = (f32[3,64,128]{2,1,0:T(8,128)S(1)}, f32[3,64,128]{2,1,0:T(8,128)S(1)}, u32[]{:S(2)}, u32[]{:S(2)}) collective-permute-start(f32[3,64,128]{2,1,0:T(8,128)S(1)} %get-tuple-element.25), channel_id=1, source_target_pairs={{0,16},{32,48},{64,80},{96,112},{128,144},{160,176},{192,208},{224... | collective-permute-start | bytes 294920 | tf_op jit(solution)/shard_map/ppermute | solution.py:278
  3.1 5.3 %collective-permute-start.1 = (f32[3,64,128]{2,1,0:T(8,128)S(1)}, f32[3,64,128]{2,1,0:T(8,128)S(1)}, u32[]{:S(2)}, u32[]{:S(2)}) collective-permute-start(f32[3,64,128]{2,1,0:T(8,128)S(1)} %get-tuple-element.26), channel_id=1, source_target_pairs={{16,32},{48,64},{80,96},{112,128},{144,160},{176,192},{208,224},{2... | collective-permute-start | bytes 294920 | tf_op jit(solution)/shard_map/ppermute | solution.py:277
  8.4 0.0 copy-done
  8.4 0.0 copy-done.1
  8.4 0.0 copy-done.2
  8.4 0.6 %shard_map.110 = (bf16[384,1024]{1,0:T(8,128)(2,1)S(1)}, bf16[128,256]{1,0:T(8,128)(2,1)S(1)}, bf16[256,256]{1,0:T(8,128)(2,1)S(1)}, bf16[256,256]{1,0:T(8,128)(...) custom-call(s32[8,128]{1,0:T(8,128)S(1)} %get-tuple-element.27.act_ref, ...), custom_call_target="tpu_custom_call" | custom-call | flops 20000000 | tf_op jit(solution)/shard_map/pallas_call | solution.py:247
  9.0 0.0 collective-permute-done.near_ref
  9.0 2.1 %collective-permute-done.1.far_ref = f32[3,64,128]{2,1,0:T(8,128)S(1)} collective-permute-done((f32[3,64,128]{2,1,0:T(8,128)S(1)}, f32[3,64,128]{2,1,0:T(8,128)S(1)}, u32[]{:S(2)}, u32[]{:S(2)}) %collective-permute-start.1) | collective-permute-done | bytes 98336 | tf_op jit(solution)/shard_map/ppermute | solution.py:277
  11.1 0.2 shard_map.111
  11.3 3.8 %collective-permute-start.2 = (f32[64,128]{1,0:T(8,128)S(1)}, f32[64,128]{1,0:T(8,128)S(1)}, u32[]{:S(2)}, u32[]{:S(2)}) collective-permute-start(f32[64,128]{1,0:T(8,128)S(1)} %get-tuple-element.32.first_ref), channel_id=1, source_target_pairs={{0,1},{2,3},{4,5},{6,7},{8,9},{10,11},{12,13},{14,15},{1,0},{3,2},... | collective-permute-start | bytes 98312 | tf_op jit(solution)/shard_map/ppermute | solution.py:290
  15.1 1.9 %collective-permute-start.3 = (f32[64,128]{1,0:T(8,128)S(1)}, f32[64,128]{1,0:T(8,128)S(1)}, u32[]{:S(2)}, u32[]{:S(2)}) collective-permute-start(f32[64,128]{1,0:T(8,128)S(1)} %get-tuple-element.33.second_ref), channel_id=1, source_target_pairs={{1,2},{3,4},{5,6},{7,8},{9,10},{11,12},{13,14},{2,1},{4,3},{6,5},{... | collective-permute-start | bytes 98312 | tf_op jit(solution)/shard_map/ppermute | solution.py:291
  17.1 0.6 %shard_map.112.moved_ref = f32[8,56,128]{2,1,0:T(8,128)S(1)} custom-call(f32[8,64,128]{2,1,0:T(8,128)S(1)} %get-tuple-element.24.all_ref, f32[3,64,128]{2,1,0:T(8,128)S(1)} %get-tuple-element.30.low_ref, f32[3,64,128]{2,1,0:T(8,128)S(1)} %get-tuple-element.31.high_ref), custom_call_target="tpu_custom_call" | custom-call | flops 20000000 | tf_op jit(solution)/shard_map/pallas_call | solution.py:247
  17.7 0.0 collective-permute-done.2.early_ref
  17.7 4.5 %collective-permute-done.3.late_ref = f32[64,128]{1,0:T(8,128)S(1)} collective-permute-done((f32[64,128]{1,0:T(8,128)S(1)}, f32[64,128]{1,0:T(8,128)S(1)}, u32[]{:S(2)}, u32[]{:S(2)}) %collective-permute-start.3) | collective-permute-done | bytes 32800 | tf_op jit(solution)/shard_map/ppermute | solution.py:291
  22.2 4.2 %shard_map.113 = f32[432,128]{1,0:T(8,128)} custom-call(f32[8,56,128]{2,1,0:T(8,128)S(1)} %shard_map.112.moved_ref, f32[64,128]{1,0:T(8,128)S(1)} %get-tuple-element.32.first_ref, f32[64,128]{1,0:T(8,128)S(1)} %get-tuple-element.33.second_ref, f32[64,128]{1,0:T(8,128)S(1)} %collective-permute-done.2.early_ref, ...), custom_call_target="tpu_custom_call" | custom-call | tf_op jit(solution)/shard_map/pallas_call | solution.py:247
Async XLA Ops:
  0.0 8.4 %copy-start = (bf16[256,256]{1,0:T(8,128)(2,1)S(1)}, bf16[256,256]{1,0:T(8,128)(2,1)}, u32[]{:S(2)}) copy-start(bf16[256,256]{1,0:T(8,128)(2,1)} %w2_ref.1) | copy-start | bytes 393220
  0.0 8.4 %copy-start.1 = (bf16[256,55]{0,1:T(8,128)(2,1)S(1)}, bf16[256,55]{0,1:T(8,128)(2,1)}, u32[]{:S(2)}) copy-start(bf16[256,55]{0,1:T(8,128)(2,1)} %param.16) | copy-start | bytes 84484
  0.0 8.4 %copy-start.2 = (bf16[54,256]{1,0:T(8,128)(2,1)S(1)}, bf16[54,256]{1,0:T(8,128)(2,1)}, u32[]{:S(2)}) copy-start(bf16[54,256]{1,0:T(8,128)(2,1)} %w3_ref.1) | copy-start | bytes 82948
  1.1 7.9 %collective-permute-start = (f32[3,64,128]{2,1,0:T(8,128)S(1)}, f32[3,64,128]{2,1,0:T(8,128)S(1)}, u32[]{:S(2)}, u32[]{:S(2)}) collective-permute-start(f32[3,64,128]{2,1,0:T(8,128)S(1)} %get-tuple-element.25), channel_id=1, source_target_pairs={{0,16},{32,48},{64,80},{96,112},{128,144},{160,176},{192,208},{224... | collective-permute-start | bytes 294920 | tf_op jit(solution)/shard_map/ppermute | solution.py:278
  3.1 8.0 %collective-permute-start.1 = (f32[3,64,128]{2,1,0:T(8,128)S(1)}, f32[3,64,128]{2,1,0:T(8,128)S(1)}, u32[]{:S(2)}, u32[]{:S(2)}) collective-permute-start(f32[3,64,128]{2,1,0:T(8,128)S(1)} %get-tuple-element.26), channel_id=1, source_target_pairs={{16,32},{48,64},{80,96},{112,128},{144,160},{176,192},{208,224},{2... | collective-permute-start | bytes 294920 | tf_op jit(solution)/shard_map/ppermute | solution.py:277
  11.3 6.3 %collective-permute-start.2 = (f32[64,128]{1,0:T(8,128)S(1)}, f32[64,128]{1,0:T(8,128)S(1)}, u32[]{:S(2)}, u32[]{:S(2)}) collective-permute-start(f32[64,128]{1,0:T(8,128)S(1)} %get-tuple-element.32.first_ref), channel_id=1, source_target_pairs={{0,1},{2,3},{4,5},{6,7},{8,9},{10,11},{12,13},{14,15},{1,0},{3,2},... | collective-permute-start | bytes 98312 | tf_op jit(solution)/shard_map/ppermute | solution.py:290
  15.1 7.0 %collective-permute-start.3 = (f32[64,128]{1,0:T(8,128)S(1)}, f32[64,128]{1,0:T(8,128)S(1)}, u32[]{:S(2)}, u32[]{:S(2)}) collective-permute-start(f32[64,128]{1,0:T(8,128)S(1)} %get-tuple-element.33.second_ref), channel_id=1, source_target_pairs={{1,2},{3,4},{5,6},{7,8},{9,10},{11,12},{13,14},{2,1},{4,3},{6,5},{... | collective-permute-start | bytes 98312 | tf_op jit(solution)/shard_map/ppermute | solution.py:291

commit v5 on v4

--- a/solution.py
+++ b/solution.py
@@ -17,6 +17,7 @@
 CHANNELS = 64
 DIFF, SPEED_C, SPEED_R, INSIDE = 54, 55, 56, 57
 WIDE = 9
+PACK = 24
 COST_PREPARE = 20_000_000
 COST_MOVE = 20_000_000
 chem_step = 0.0625
@@ -55,7 +56,25 @@
         far_ref[k] = jnp.where(odd, bottom, top)
 
 
-def strip_kernel(all_ref, near_ref, far_ref, token_ref, low_ref, high_ref, first_ref, second_ref):
+def packed(strip, place, at):
+    total = strip[0:PACK]
+    for k in (1, 2):
+        part = strip[PACK * k : PACK * (k + 1)] if k == 1 else jnp.concatenate([strip[2 * PACK :], strip[0:8]], 0)
+        step = 3 * k if at == 0 else -3 * k
+        lo = (at + step) % WIDE
+        total = jnp.where((place >= lo) & (place < lo + 3), pltpu.roll(part, step % LANES, 1), total)
+    return total
+
+
+def unpacked(pack, at):
+    parts = [pack]
+    for k in (1, 2):
+        step = -3 * k if at == 0 else 3 * k
+        parts.append(pltpu.roll(pack, step % LANES, 1))
+    return jnp.concatenate(parts, 0)[0:CHANNELS]
+
+
+def strip_kernel(all_ref, near_ref, far_ref, token_ref, low_ref, high_ref, left_ref, right_ref, first_ref, second_ref):
     odd = lax.axis_index("row") % 2 == 1
     for k in range(STEPS):
         near, far = near_ref[k], far_ref[k]
@@ -72,6 +91,11 @@
         hit = (lane - at) % LANES < WIDE
         right = jnp.where(hit, pltpu.roll(plane, (at + 6) % LANES, 1), right)
     odd = lax.axis_index("col") % 2 == 1
+    left_ref[...] = left
+    right_ref[...] = right
+    place = iota((PACK, LANES), 1)
+    left = packed(left, place % WIDE, 0)
+    right = packed(right, (place + 3) % LANES % WIDE, 6)
     first_ref[...] = jnp.where(odd, right, left)
     second_ref[...] = jnp.where(odd, left, right)
 
@@ -181,16 +205,16 @@
 
 
 def main_kernel(
-    moved_ref, first_ref, second_ref, early_ref, late_ref,
+    moved_ref, left_own, right_own, early_ref, late_ref,
     pick_ref, w1t_ref, w2t_ref, mix_ref, w3t_ref, bias_ref, b1_ref, b2_ref, b3_ref, heat_ref,
     out_ref, full_ref, feat_ref, pre_ref, sum_ref,
 ):
     lane = iota((CHANNELS, LANES), 1)
     odd = lax.axis_index("col") % 2 == 1
-    first, second, early, late = first_ref[...], second_ref[...], early_ref[...], late_ref[...]
-    left = jnp.where(lane % WIDE < 3, jnp.where(odd, early, late), jnp.where(odd, second, first))
+    early, late = early_ref[...], late_ref[...]
+    left = jnp.where(lane % WIDE < 3, unpacked(jnp.where(odd, early, late), 0), left_own[...])
     inner = (lane + 3) % LANES % WIDE < 6
-    right = jnp.where(inner, jnp.where(odd, first, second), jnp.where(odd, late, early))
+    right = jnp.where(inner, right_own[...], unpacked(jnp.where(odd, late, early), 6))
     left, right = move_strip(left), move_strip(right)
     lane = iota((56, LANES), 1)
     place = lane % WIDE
@@ -285,7 +309,10 @@
         (active, w1.T, w2, w3, b3),
         cost=COST_PREPARE,
     )
-    low, high, first, second = call(strip_kernel, [edge, edge, (plane, f32), (plane, f32)], (every, near, far, token))
+    pack = ((PACK, LANES), f32)
+    low, high, left_own, right_own, first, second = call(
+        strip_kernel, [edge, edge, (plane, f32), (plane, f32), pack, pack], (every, near, far, token)
+    )
     devices = lax.axis_size("col")
     early = lax.ppermute(first, "col", swaps(devices, 0))
     late = lax.ppermute(second, "col", swaps(devices, 1))
@@ -297,7 +324,7 @@
     (out,) = call(
         main_kernel,
         [((KINDS * ROWS, LANES), f32)],
-        (moved, first, second, early, late, *picks, b1, b2, b3, heat),
+        (moved, left_own, right_own, early, late, *picks, b1, b2, b3, heat),
         scratch=[
             ((ROWS, 56, LANES), f32), ((2 * CHANNELS, ROWS * LANES), bf16), ((CAP, HID), f32), ((CAP, HID), f32),
         ],

time: 26.5 us -> 26.4 us (level)
  the two profiles are of different devices: /device:TPU:134 before, /device:TPU:130 now
where the time goes in v5:
time: 26.4 us; the launch traced here: 26.2 us
  starting transfers between devices  12.7 us (48%)
  Pallas kernels  6.78 us (26%)
  waiting for transfers between devices  6.69 us (25%)
    pallas_call x5, Pallas kernels, call(): pl.pallas_call(kernel, out_shape=[jax.ShapeDtypeStruct(s, t) for s, t in...  6.78 us
    ppermute x1, starting transfers between devices, shards(): far = lax.ppermute(far, 'row', swaps(devices, 1))  5 us
    ppermute x1, waiting for transfers between devices, shards(): late = lax.ppermute(second, 'col', swaps(devices, 1))  4.28 us
    ppermute x1, starting transfers between devices, shards(): early = lax.ppermute(first, 'col', swaps(devices, 0))  3.83 us
    ppermute x1, waiting for transfers between devices, shards(): far = lax.ppermute(far, 'row', swaps(devices, 1))  2.41 us
    ppermute x1, starting transfers between devices, shards(): near = lax.ppermute(near, 'row', swaps(devices, 0))  1.92 us
    ppermute x1, starting transfers between devices, shards(): late = lax.ppermute(second, 'col', swaps(devices, 1))  1.92 us
  transfers between devices with their start and end apart: 4, of which 2 were waited for; matrix products, arithmetic and copies ran while one was open for 0% of the time, Pallas kernels for 4%

profile of v5, /device:TPU:130, one launch (start us, length us, event | category | flops | bytes accessed | tf_op | source)
XLA Modules:
  0.0 26.2 jit_solution(11217133486207243079)
XLA Ops:
  0.0 0.0 copy-start
  0.0 0.0 copy-start.1
  0.0 0.0 copy-start.2
  0.0 1.1 %shard_map.109 = (f32[8,64,128]{2,1,0:T(8,128)S(1)}, f32[3,64,128]{2,1,0:T(8,128)S(1)}, f32[3,64,128]{2,1,0:T(8,128)S(1)}, s32[8,128]{1,0:T(8,128)S(1)}, f32[8,1...) custom-call(f32[432,128]{1,0:T(8,128)} %bitcast.7, f32[8,128]{1,0:T(8,128)} %d_hbm.1, ...), custom_call_target="tpu_custom_call" | custom-call | tf_op jit(solution)/shard_map/pallas_call | solution.py:271
  1.1 1.9 %collective-permute-start = (f32[3,64,128]{2,1,0:T(8,128)S(1)}, f32[3,64,128]{2,1,0:T(8,128)S(1)}, u32[]{:S(2)}, u32[]{:S(2)}) collective-permute-start(f32[3,64,128]{2,1,0:T(8,128)S(1)} %get-tuple-element.27), channel_id=1, source_target_pairs={{0,16},{32,48},{64,80},{96,112},{128,144},{160,176},{192,208},{224... | collective-permute-start | bytes 294920 | tf_op jit(solution)/shard_map/ppermute | solution.py:302
  3.1 5.0 %collective-permute-start.1 = (f32[3,64,128]{2,1,0:T(8,128)S(1)}, f32[3,64,128]{2,1,0:T(8,128)S(1)}, u32[]{:S(2)}, u32[]{:S(2)}) collective-permute-start(f32[3,64,128]{2,1,0:T(8,128)S(1)} %get-tuple-element.28), channel_id=1, source_target_pairs={{16,32},{48,64},{80,96},{112,128},{144,160},{176,192},{208,224},{2... | collective-permute-start | bytes 294920 | tf_op jit(solution)/shard_map/ppermute | solution.py:301
  8.1 0.0 copy-done
  8.1 0.0 copy-done.1
  8.1 0.0 copy-done.2
  8.1 0.6 %shard_map.110 = (bf16[384,1024]{1,0:T(8,128)(2,1)S(1)}, bf16[128,256]{1,0:T(8,128)(2,1)S(1)}, bf16[256,256]{1,0:T(8,128)(2,1)S(1)}, bf16[256,256]{1,0:T(8,128)(...) custom-call(s32[8,128]{1,0:T(8,128)S(1)} %get-tuple-element.29.act_ref, ...), custom_call_target="tpu_custom_call" | custom-call | flops 20000000 | tf_op jit(solution)/shard_map/pallas_call | solution.py:271
  8.7 0.0 collective-permute-done.near_ref
  8.7 2.4 %collective-permute-done.1.far_ref = f32[3,64,128]{2,1,0:T(8,128)S(1)} collective-permute-done((f32[3,64,128]{2,1,0:T(8,128)S(1)}, f32[3,64,128]{2,1,0:T(8,128)S(1)}, u32[]{:S(2)}, u32[]{:S(2)}) %collective-permute-start.1) | collective-permute-done | bytes 98336 | tf_op jit(solution)/shard_map/ppermute | solution.py:301
  11.1 0.3 shard_map.111
  11.4 3.8 %collective-permute-start.2 = (f32[24,128]{1,0:T(8,128)S(1)}, f32[24,128]{1,0:T(8,128)S(1)}, u32[]{:S(2)}, u32[]{:S(2)}) collective-permute-start(f32[24,128]{1,0:T(8,128)S(1)} %get-tuple-element.36), channel_id=1, source_target_pairs={{0,1},{2,3},{4,5},{6,7},{8,9},{10,11},{12,13},{14,15},{1,0},{3,2},... | collective-permute-start | bytes 36872 | tf_op jit(solution)/shard_map/ppermute | solution.py:317
  15.2 1.9 %collective-permute-start.3 = (f32[24,128]{1,0:T(8,128)S(1)}, f32[24,128]{1,0:T(8,128)S(1)}, u32[]{:S(2)}, u32[]{:S(2)}) collective-permute-start(f32[24,128]{1,0:T(8,128)S(1)} %get-tuple-element.37), channel_id=1, source_target_pairs={{1,2},{3,4},{5,6},{7,8},{9,10},{11,12},{13,14},{2,1},{4,3},{6,5},{... | collective-permute-start | bytes 36872 | tf_op jit(solution)/shard_map/ppermute | solution.py:318
  17.1 0.6 %shard_map.112.moved_ref = f32[8,56,128]{2,1,0:T(8,128)S(1)} custom-call(f32[8,64,128]{2,1,0:T(8,128)S(1)} %get-tuple-element.26.all_ref, f32[3,64,128]{2,1,0:T(8,128)S(1)} %get-tuple-element.32.low_ref, f32[3,64,128]{2,1,0:T(8,128)S(1)} %get-tuple-element.33.high_ref), custom_call_target="tpu_custom_call" | custom-call | flops 20000000 | tf_op jit(solution)/shard_map/pallas_call | solution.py:271
  17.7 0.0 collective-permute-done.2.early_ref
  17.7 4.3 %collective-permute-done.3.late_ref = f32[24,128]{1,0:T(8,128)S(1)} collective-permute-done((f32[24,128]{1,0:T(8,128)S(1)}, f32[24,128]{1,0:T(8,128)S(1)}, u32[]{:S(2)}, u32[]{:S(2)}) %collective-permute-start.3) | collective-permute-done | bytes 12320 | tf_op jit(solution)/shard_map/ppermute | solution.py:318
  22.0 4.2 %shard_map.113 = f32[432,128]{1,0:T(8,128)} custom-call(f32[8,56,128]{2,1,0:T(8,128)S(1)} %shard_map.112.moved_ref, f32[64,128]{1,0:T(8,128)S(1)} %get-tuple-element.34.left_own, f32[64,128]{1,0:T(8,128)S(1)} %get-tuple-element.35.right_own, f32[24,128]{1,0:T(8,128)S(1)} %collective-permute-done.2.early_ref, f32[24,128]{1,0:T(8,128)S(1)} %collective-permute-done.3.late_ref, ...), custom_call_target="tpu_custom_call" | custom-call | tf_op jit(solution)/shard_map/pallas_call | solution.py:271
Async XLA Ops:
  0.0 8.1 %copy-start = (bf16[256,256]{1,0:T(8,128)(2,1)S(1)}, bf16[256,256]{1,0:T(8,128)(2,1)}, u32[]{:S(2)}) copy-start(bf16[256,256]{1,0:T(8,128)(2,1)} %w2_ref.1) | copy-start | bytes 393220
  0.0 8.1 %copy-start.1 = (bf16[256,55]{0,1:T(8,128)(2,1)S(1)}, bf16[256,55]{0,1:T(8,128)(2,1)}, u32[]{:S(2)}) copy-start(bf16[256,55]{0,1:T(8,128)(2,1)} %param.16) | copy-start | bytes 84484
  0.0 8.1 %copy-start.2 = (bf16[54,256]{1,0:T(8,128)(2,1)S(1)}, bf16[54,256]{1,0:T(8,128)(2,1)}, u32[]{:S(2)}) copy-start(bf16[54,256]{1,0:T(8,128)(2,1)} %w3_ref.1) | copy-start | bytes 82948
  1.1 7.6 %collective-permute-start = (f32[3,64,128]{2,1,0:T(8,128)S(1)}, f32[3,64,128]{2,1,0:T(8,128)S(1)}, u32[]{:S(2)}, u32[]{:S(2)}) collective-permute-start(f32[3,64,128]{2,1,0:T(8,128)S(1)} %get-tuple-element.27), channel_id=1, source_target_pairs={{0,16},{32,48},{64,80},{96,112},{128,144},{160,176},{192,208},{224... | collective-permute-start | bytes 294920 | tf_op jit(solution)/shard_map/ppermute | solution.py:302
  3.1 8.0 %collective-permute-start.1 = (f32[3,64,128]{2,1,0:T(8,128)S(1)}, f32[3,64,128]{2,1,0:T(8,128)S(1)}, u32[]{:S(2)}, u32[]{:S(2)}) collective-permute-start(f32[3,64,128]{2,1,0:T(8,128)S(1)} %get-tuple-element.28), channel_id=1, source_target_pairs={{16,32},{48,64},{80,96},{112,128},{144,160},{176,192},{208,224},{2... | collective-permute-start | bytes 294920 | tf_op jit(solution)/shard_map/ppermute | solution.py:301
  11.4 6.3 %collective-permute-start.2 = (f32[24,128]{1,0:T(8,128)S(1)}, f32[24,128]{1,0:T(8,128)S(1)}, u32[]{:S(2)}, u32[]{:S(2)}) collective-permute-start(f32[24,128]{1,0:T(8,128)S(1)} %get-tuple-element.36), channel_id=1, source_target_pairs={{0,1},{2,3},{4,5},{6,7},{8,9},{10,11},{12,13},{14,15},{1,0},{3,2},... | collective-permute-start | bytes 36872 | tf_op jit(solution)/shard_map/ppermute | solution.py:317
  15.2 6.8 %collective-permute-start.3 = (f32[24,128]{1,0:T(8,128)S(1)}, f32[24,128]{1,0:T(8,128)S(1)}, u32[]{:S(2)}, u32[]{:S(2)}) collective-permute-start(f32[24,128]{1,0:T(8,128)S(1)} %get-tuple-element.37), channel_id=1, source_target_pairs={{1,2},{3,4},{5,6},{7,8},{9,10},{11,12},{13,14},{2,1},{4,3},{6,5},{... | collective-permute-start | bytes 36872 | tf_op jit(solution)/shard_map/ppermute | solution.py:318

commit v6 on v4

--- a/solution.py
+++ b/solution.py
@@ -77,7 +77,7 @@
 
 
 def prepare_kernel(
-    act_ref, w1_ref, w2_ref, w3_ref, b3_ref, pick_ref, w1t_ref, w2t_ref, mix_ref, w3t_ref, bias_ref, token_ref
+    act_ref, w1_ref, w2_ref, w3_ref, b3_ref, pick_ref, w1t_ref, w2t_ref, mix_ref, w3p_ref, bias_ref, shift_ref, token_ref
 ):
     token_ref[...] = jnp.zeros(token_ref.shape, f32)
     act = act_ref[...].astype(f32)
@@ -99,7 +99,8 @@
         w1t_ref[k * CHANNELS : k * CHANNELS + KINDS + 1, :] = w1t.astype(bf16)
     w2t_ref[...] = w2_ref[...].astype(f32).T.astype(bf16)
     w3t = w3_ref[...].astype(f32).T
-    w3t_ref[...] = w3t.astype(bf16)
+    w3p_ref[...] = jnp.zeros((CHANNELS, HID), bf16)
+    w3p_ref[0:KINDS, :] = w3_ref[...]
     part = w1t[0:KINDS, :]
     mix = jnp.dot(w3t.astype(bf16), part.astype(bf16), preferred_element_type=f32)
     mix_ref[...] = (chem_step * mix).astype(bf16)
@@ -107,6 +108,8 @@
     same = iota((KINDS, KINDS), 0) == iota((KINDS, KINDS), 1)
     shifts = jnp.sum(jnp.where(same, shifts, 0.0), axis=1, keepdims=True)
     bias_ref[...] = chem_step * jnp.sum(part * shifts, axis=0, keepdims=True)
+    shift_ref[...] = jnp.zeros((CHANNELS, LANES), f32)
+    shift_ref[0:KINDS, :] = jnp.broadcast_to(SUBSTEPS * shifts, (KINDS, LANES))
 
 
 def face(d_low, d_high, u_low, u_high):
@@ -182,7 +185,7 @@
 
 def main_kernel(
     moved_ref, first_ref, second_ref, early_ref, late_ref,
-    pick_ref, w1t_ref, w2t_ref, mix_ref, w3t_ref, bias_ref, b1_ref, b2_ref, b3_ref, heat_ref,
+    pick_ref, w1t_ref, w2t_ref, mix_ref, w3p_ref, bias_ref, shift_ref, b1_ref, b2_ref, heat_ref,
     out_ref, full_ref, feat_ref, pre_ref, sum_ref,
 ):
     lane = iota((CHANNELS, LANES), 1)
@@ -225,9 +228,9 @@
     total = sum_ref[...]
     high = total.astype(bf16)
     low = (total - high.astype(f32)).astype(bf16)
-    rate = jnp.dot(high, w3t_ref[...], preferred_element_type=f32) + jnp.dot(low, w3t_ref[...], preferred_element_type=f32)
-    rate = chem_step * (rate + SUBSTEPS * b3_ref[...])
-    rate = jnp.concatenate([rate, jnp.zeros((CAP, LANES - KINDS), f32)], 1).T[0:CHANNELS, :]
+    turned = lambda x: lax.dot_general(w3p_ref[...], x, (((1,), (1,)), ((), ())), preferred_element_type=f32)
+    rate = turned(high) + turned(low)
+    rate = chem_step * (rate + jnp.concatenate([shift_ref[...]] * (CAP // LANES), 1))
     high = rate.astype(bf16)
     low = (rate - high.astype(f32)).astype(bf16)
     both = jnp.concatenate([high, low], 0)
@@ -280,7 +283,7 @@
         prepare_kernel,
         [
             ((CAP, ROWS * LANES), bf16), ((2 * CHANNELS, HID), bf16), ((HID, HID), bf16), ((HID, HID), bf16),
-            ((HID, KINDS), bf16), ((1, HID), f32), (tile, f32),
+            ((CHANNELS, HID), bf16), ((1, HID), f32), (plane, f32), (tile, f32),
         ],
         (active, w1.T, w2, w3, b3),
         cost=COST_PREPARE,
@@ -297,7 +300,7 @@
     (out,) = call(
         main_kernel,
         [((KINDS * ROWS, LANES), f32)],
-        (moved, first, second, early, late, *picks, b1, b2, b3, heat),
+        (moved, first, second, early, late, *picks, b1, b2, heat),
         scratch=[
             ((ROWS, 56, LANES), f32), ((2 * CHANNELS, ROWS * LANES), bf16), ((CAP, HID), f32), ((CAP, HID), f32),
         ],

time: 26.5 us -> 26.6 us (level)
  the two profiles are of different devices: /device:TPU:134 before, /device:TPU:130 now
where the time goes in v6:
time: 26.6 us; the launch traced here: 26.4 us
  starting transfers between devices  12.7 us (48%)
  waiting for transfers between devices  6.91 us (26%)
  Pallas kernels  6.66 us (25%)
    pallas_call x5, Pallas kernels, call(): pl.pallas_call(kernel, out_shape=[jax.ShapeDtypeStruct(s, t) for s, t in...  6.66 us
    ppermute x1, starting transfers between devices, shards(): far = lax.ppermute(far, 'row', swaps(devices, 1))  5 us
    ppermute x1, waiting for transfers between devices, shards(): late = lax.ppermute(second, 'col', swaps(devices, 1))  4.5 us
    ppermute x1, starting transfers between devices, shards(): early = lax.ppermute(first, 'col', swaps(devices, 0))  3.83 us
    ppermute x1, waiting for transfers between devices, shards(): far = lax.ppermute(far, 'row', swaps(devices, 1))  2.41 us
    ppermute x1, starting transfers between devices, shards(): near = lax.ppermute(near, 'row', swaps(devices, 0))  1.92 us
    ppermute x1, starting transfers between devices, shards(): late = lax.ppermute(second, 'col', swaps(devices, 1))  1.92 us
  transfers between devices with their start and end apart: 4, of which 2 were waited for; matrix products, arithmetic and copies ran while one was open for 0% of the time, Pallas kernels for 4%

profile of v6, /device:TPU:130, one launch (start us, length us, event | category | flops | bytes accessed | tf_op | source)
XLA Modules:
  0.0 26.4 jit_solution(4519407208800926779)
XLA Ops:
  0.0 0.0 copy-start
  0.0 0.0 copy-start.1
  0.0 0.0 copy-start.2
  0.0 1.1 %shard_map.109 = (f32[8,64,128]{2,1,0:T(8,128)S(1)}, f32[3,64,128]{2,1,0:T(8,128)S(1)}, f32[3,64,128]{2,1,0:T(8,128)S(1)}, s32[8,128]{1,0:T(8,128)S(1)}, f32[8,1...) custom-call(f32[432,128]{1,0:T(8,128)} %bitcast.7, f32[8,128]{1,0:T(8,128)} %d_hbm.1, ...), custom_call_target="tpu_custom_call" | custom-call | tf_op jit(solution)/shard_map/pallas_call | solution.py:250
  1.1 1.9 %collective-permute-start = (f32[3,64,128]{2,1,0:T(8,128)S(1)}, f32[3,64,128]{2,1,0:T(8,128)S(1)}, u32[]{:S(2)}, u32[]{:S(2)}) collective-permute-start(f32[3,64,128]{2,1,0:T(8,128)S(1)} %get-tuple-element.26), channel_id=1, source_target_pairs={{0,16},{32,48},{64,80},{96,112},{128,144},{160,176},{192,208},{224... | collective-permute-start | bytes 294920 | tf_op jit(solution)/shard_map/ppermute | solution.py:281
  3.1 5.0 %collective-permute-start.1 = (f32[3,64,128]{2,1,0:T(8,128)S(1)}, f32[3,64,128]{2,1,0:T(8,128)S(1)}, u32[]{:S(2)}, u32[]{:S(2)}) collective-permute-start(f32[3,64,128]{2,1,0:T(8,128)S(1)} %get-tuple-element.27), channel_id=1, source_target_pairs={{16,32},{48,64},{80,96},{112,128},{144,160},{176,192},{208,224},{2... | collective-permute-start | bytes 294920 | tf_op jit(solution)/shard_map/ppermute | solution.py:280
  8.1 0.0 copy-done
  8.1 0.0 copy-done.1
  8.1 0.0 copy-done.2
  8.1 0.6 %shard_map.110 = (bf16[384,1024]{1,0:T(8,128)(2,1)S(1)}, bf16[128,256]{1,0:T(8,128)(2,1)S(1)}, bf16[256,256]{1,0:T(8,128)(2,1)S(1)}, bf16[256,256]{1,0:T(8,128)(...) custom-call(s32[8,128]{1,0:T(8,128)S(1)} %get-tuple-element.28.act_r, ...), custom_call_target="tpu_custom_call" | custom-call | flops 20000000 | tf_op jit(solution)/shard_map/pallas_call | solution.py:250
  8.7 0.0 collective-permute-done.near_ref
  8.7 2.4 %collective-permute-done.1.far_ref = f32[3,64,128]{2,1,0:T(8,128)S(1)} collective-permute-done((f32[3,64,128]{2,1,0:T(8,128)S(1)}, f32[3,64,128]{2,1,0:T(8,128)S(1)}, u32[]{:S(2)}, u32[]{:S(2)}) %collective-permute-start.1) | collective-permute-done | bytes 98336 | tf_op jit(solution)/shard_map/ppermute | solution.py:280
  11.1 0.2 shard_map.111
  11.3 3.8 %collective-permute-start.2 = (f32[64,128]{1,0:T(8,128)S(1)}, f32[64,128]{1,0:T(8,128)S(1)}, u32[]{:S(2)}, u32[]{:S(2)}) collective-permute-start(f32[64,128]{1,0:T(8,128)S(1)} %get-tuple-element.33.first_ref), channel_id=1, source_target_pairs={{0,1},{2,3},{4,5},{6,7},{8,9},{10,11},{12,13},{14,15},{1,0},{3,2},... | collective-permute-start | bytes 98312 | tf_op jit(solution)/shard_map/ppermute | solution.py:293
  15.1 1.9 %collective-permute-start.3 = (f32[64,128]{1,0:T(8,128)S(1)}, f32[64,128]{1,0:T(8,128)S(1)}, u32[]{:S(2)}, u32[]{:S(2)}) collective-permute-start(f32[64,128]{1,0:T(8,128)S(1)} %get-tuple-element.34.second_ref), channel_id=1, source_target_pairs={{1,2},{3,4},{5,6},{7,8},{9,10},{11,12},{13,14},{2,1},{4,3},{6,5},{... | collective-permute-start | bytes 98312 | tf_op jit(solution)/shard_map/ppermute | solution.py:294
  17.1 0.6 %shard_map.112.moved_ref = f32[8,56,128]{2,1,0:T(8,128)S(1)} custom-call(f32[8,64,128]{2,1,0:T(8,128)S(1)} %get-tuple-element.25.all_ref, f32[3,64,128]{2,1,0:T(8,128)S(1)} %get-tuple-element.31.low_ref, f32[3,64,128]{2,1,0:T(8,128)S(1)} %get-tuple-element.32.high_ref), custom_call_target="tpu_custom_call" | custom-call | flops 20000000 | tf_op jit(solution)/shard_map/pallas_call | solution.py:250
  17.7 0.0 collective-permute-done.2.early_ref
  17.7 4.5 %collective-permute-done.3.late_ref = f32[64,128]{1,0:T(8,128)S(1)} collective-permute-done((f32[64,128]{1,0:T(8,128)S(1)}, f32[64,128]{1,0:T(8,128)S(1)}, u32[]{:S(2)}, u32[]{:S(2)}) %collective-permute-start.3) | collective-permute-done | bytes 32800 | tf_op jit(solution)/shard_map/ppermute | solution.py:294
  22.2 4.2 %shard_map.113 = f32[432,128]{1,0:T(8,128)} custom-call(f32[8,56,128]{2,1,0:T(8,128)S(1)} %shard_map.112.moved_ref, f32[64,128]{1,0:T(8,128)S(1)} %get-tuple-element.33.first_ref, f32[64,128]{1,0:T(8,128)S(1)} %get-tuple-element.34.second_ref, f32[64,128]{1,0:T(8,128)S(1)} %collective-permute-done.2.early_ref, ...), custom_call_target="tpu_custom_call" | custom-call | tf_op jit(solution)/shard_map/pallas_call | solution.py:250
Async XLA Ops:
  0.0 8.1 %copy-start = (bf16[256,256]{1,0:T(8,128)(2,1)S(1)}, bf16[256,256]{1,0:T(8,128)(2,1)}, u32[]{:S(2)}) copy-start(bf16[256,256]{1,0:T(8,128)(2,1)} %w2_ref.1) | copy-start | bytes 393220
  0.0 8.1 %copy-start.1 = (bf16[256,55]{0,1:T(8,128)(2,1)S(1)}, bf16[256,55]{0,1:T(8,128)(2,1)}, u32[]{:S(2)}) copy-start(bf16[256,55]{0,1:T(8,128)(2,1)} %param.16) | copy-start | bytes 84484
  0.0 8.1 %copy-start.2 = (bf16[54,256]{1,0:T(8,128)(2,1)S(1)}, bf16[54,256]{1,0:T(8,128)(2,1)}, u32[]{:S(2)}) copy-start(bf16[54,256]{1,0:T(8,128)(2,1)} %w3_ref.1) | copy-start | bytes 82948
  1.1 7.6 %collective-permute-start = (f32[3,64,128]{2,1,0:T(8,128)S(1)}, f32[3,64,128]{2,1,0:T(8,128)S(1)}, u32[]{:S(2)}, u32[]{:S(2)}) collective-permute-start(f32[3,64,128]{2,1,0:T(8,128)S(1)} %get-tuple-element.26), channel_id=1, source_target_pairs={{0,16},{32,48},{64,80},{96,112},{128,144},{160,176},{192,208},{224... | collective-permute-start | bytes 294920 | tf_op jit(solution)/shard_map/ppermute | solution.py:281
  3.1 8.0 %collective-permute-start.1 = (f32[3,64,128]{2,1,0:T(8,128)S(1)}, f32[3,64,128]{2,1,0:T(8,128)S(1)}, u32[]{:S(2)}, u32[]{:S(2)}) collective-permute-start(f32[3,64,128]{2,1,0:T(8,128)S(1)} %get-tuple-element.27), channel_id=1, source_target_pairs={{16,32},{48,64},{80,96},{112,128},{144,160},{176,192},{208,224},{2... | collective-permute-start | bytes 294920 | tf_op jit(solution)/shard_map/ppermute | solution.py:280
  11.3 6.3 %collective-permute-start.2 = (f32[64,128]{1,0:T(8,128)S(1)}, f32[64,128]{1,0:T(8,128)S(1)}, u32[]{:S(2)}, u32[]{:S(2)}) collective-permute-start(f32[64,128]{1,0:T(8,128)S(1)} %get-tuple-element.33.first_ref), channel_id=1, source_target_pairs={{0,1},{2,3},{4,5},{6,7},{8,9},{10,11},{12,13},{14,15},{1,0},{3,2},... | collective-permute-start | bytes 98312 | tf_op jit(solution)/shard_map/ppermute | solution.py:293
  15.1 7.0 %collective-permute-start.3 = (f32[64,128]{1,0:T(8,128)S(1)}, f32[64,128]{1,0:T(8,128)S(1)}, u32[]{:S(2)}, u32[]{:S(2)}) collective-permute-start(f32[64,128]{1,0:T(8,128)S(1)} %get-tuple-element.34.second_ref), channel_id=1, source_target_pairs={{1,2},{3,4},{5,6},{7,8},{9,10},{11,12},{13,14},{2,1},{4,3},{6,5},{... | collective-permute-start | bytes 98312 | tf_op jit(solution)/shard_map/ppermute | solution.py:294
